TPU v7x, 128 devices: a whole 4x4x4 slice. The times are simulated.
128 devices in a mesh: ctx: 32 (over y, z, core), tp: 4 (over x).
Axes of the slice: x: 4, y: 4, z: 4, core: 2. Of those that a mesh axis runs over, the one named last changes fastest.
Arguments:
- tokens: bfloat16 [4096, 4096], P('ctx', 'tp'), may hold values from -6 to 6
- out_grad: bfloat16 [4096, 4096], P('ctx', 'tp'), may hold values from -4 to 4
- router_probs: bfloat16 [4096, 8], P('ctx'), may hold values from 0.049804688 to 0.5
- expert_ids: int32 [4096, 8], P('ctx'), may hold values from 0 to 63, all different within a row; in each aligned block of 128 rows (0 to 127, 128 to 255, ...) at most 24 rows name the same one
- w_gate: bfloat16 [64, 4096, 1536], P('ctx', None, 'tp'), may hold values from -0.09375 to 0.09375
- w_up: bfloat16 [64, 4096, 1536], P('ctx', None, 'tp'), may hold values from -0.09375 to 0.09375
- w_down: bfloat16 [64, 1536, 4096], P('ctx', 'tp'), may hold values from -0.15625 to 0.15625
Outputs:
- token_grad: bfloat16 [4096, 4096], P('ctx', 'tp')
- prob_grad: bfloat16 [4096, 8], P('ctx')
Inputs may be any that keep to these rules, and one draw needn't show every extreme that they name: `expert_ids`: each token names 8 different experts; among the 128 tokens of one index of ctx no expert is named by more than 24 tokens, a bound that some block reaches.
All inputs are finite; a program needn't handle non-finite values.
Results may differ from a plain program's by a relative error of at most 0.015.
Values may be sent and summed in bfloat16 or wider, within the bound.
A program may use at most 128 MiB of HBM per device.

v0:
```python
import jax
import jax.numpy as jnp
from jax import lax
from jax.sharding import PartitionSpec as P


def on_device(tokens, out_grad, router_probs, expert_ids, w_gate, w_up, w_down):
    groups = lax.axis_size("ctx")
    tok_rows, fanout = expert_ids.shape
    local_experts = w_gate.shape[0]
    experts_all = local_experts * groups
    capacity = 3 * tok_rows * fanout // (2 * experts_all)
    buffer_rows = experts_all * capacity
    flat_ids = expert_ids.reshape(tok_rows * fanout)
    expert_hot = (flat_ids[:, None] == jnp.arange(experts_all, dtype=jnp.int32)[None, :]).astype(
        jnp.int32
    )
    earlier = jnp.cumsum(expert_hot, axis=0) - expert_hot
    slot_index = jnp.sum(earlier * expert_hot, axis=1)
    target = flat_ids * capacity + slot_index
    row_hot = (target[:, None] == jnp.arange(buffer_rows, dtype=jnp.int32)[None, :]).astype(
        jnp.bfloat16
    )
    row_hot = row_hot.reshape(tok_rows, fanout, buffer_rows)
    selector = jnp.sum(row_hot, axis=1)
    prob_send = jnp.einsum("tkr,tk->r", row_hot, router_probs, preferred_element_type=jnp.float32)
    prob_send = prob_send.astype(jnp.bfloat16).reshape(groups, local_experts, capacity)

    def arrange(local_rows):
        placed = jnp.einsum("tr,td->rd", selector, local_rows, preferred_element_type=jnp.float32)
        return placed.astype(jnp.bfloat16).reshape(
            groups, local_experts, capacity, local_rows.shape[1]
        )

    full_tokens, full_grads = (
        lax.all_gather(tokens, "tp", axis=1, tiled=True),
        lax.all_gather(out_grad, "tp", axis=1, tiled=True),
    )
    x_rows, dy_rows, prob_rows = (
        lax.all_to_all(arrange(full_tokens), "ctx", split_axis=0, concat_axis=0, tiled=True),
        lax.all_to_all(arrange(full_grads), "ctx", split_axis=0, concat_axis=0, tiled=True),
        lax.all_to_all(prob_send, "ctx", split_axis=0, concat_axis=0, tiled=True),
    )
    gate_sum = jnp.einsum("secd,edf->secf", x_rows, w_gate, preferred_element_type=jnp.float32)
    up_sum = jnp.einsum("secd,edf->secf", x_rows, w_up, preferred_element_type=jnp.float32)
    down_back = jnp.einsum("secd,efd->secf", dy_rows, w_down, preferred_element_type=jnp.float32)
    sigmoid_gate = jax.nn.sigmoid(gate_sum)
    gated = gate_sum * sigmoid_gate
    hidden = gated * up_sum
    prob_part = jnp.sum(hidden * down_back, axis=3)
    prob_total = lax.psum(prob_part, "tp")
    hidden_grad = prob_rows.astype(jnp.float32)[..., None] * down_back
    gate_grad = (
        hidden_grad * up_sum * sigmoid_gate * (1.0 + gate_sum * (1.0 - sigmoid_gate))
    ).astype(jnp.bfloat16)
    up_grad = (hidden_grad * gated).astype(jnp.bfloat16)
    row_part = jnp.einsum("secf,edf->secd", gate_grad, w_gate, preferred_element_type=jnp.float32)
    row_part = row_part + jnp.einsum(
        "secf,edf->secd", up_grad, w_up, preferred_element_type=jnp.float32
    )
    row_grads = lax.psum_scatter(
        row_part.astype(jnp.bfloat16), "tp", scatter_dimension=3, tiled=True
    )
    back_rows, back_probs = (
        lax.all_to_all(row_grads, "ctx", split_axis=0, concat_axis=0, tiled=True),
        lax.all_to_all(
            prob_total.astype(jnp.bfloat16), "ctx", split_axis=0, concat_axis=0, tiled=True
        ),
    )
    token_grad = jnp.einsum(
        "tr,rd->td",
        selector,
        back_rows.reshape(buffer_rows, back_rows.shape[3]),
        preferred_element_type=jnp.float32,
    )
    prob_grad = back_probs.reshape(buffer_rows)[target].reshape(tok_rows, fanout)
    return (token_grad.astype(jnp.bfloat16), prob_grad)


def solution(mesh):
    return jax.shard_map(
        on_device,
        mesh=mesh,
        in_specs=(
            P("ctx", "tp"),
            P("ctx", "tp"),
            P("ctx", None),
            P("ctx", None),
            P("ctx", None, "tp"),
            P("ctx", None, "tp"),
            P("ctx", "tp", None),
        ),
        out_specs=(P("ctx", "tp"), P("ctx", None)),
        check_vma=False,
    )
```

profile of v0, /device:TPU:0, one launch (start us, length us, event | category | flops | bytes accessed | tf_op | source)
XLA Modules:
  0.0 694.2 jit_solution(9516662253684740646)
XLA Ops:
  7.2 0.0 all-gather.5.cloned.1.call-start
  7.2 0.7 all-gather.5.cloned.1.call-update
  7.9 0.8 copy.72
  8.7 0.1 eq.44
  8.8 0.1 eq.40
  8.9 0.8 copy.86
  9.7 18.0 %reduce-window.6 = s32[64,8,128]{2,1,0:T(8,128)S(1)} reduce-window(s32[64,8,128]{2,1,0:T(8,128)S(1)} %fusion.34, s32[]{:T(128)} %constant.4.clone.1), window={size=1x1x128 pad=0_0x0_0x127_0}, to_apply=%region_0.0 | reduce-window | flops 8323072 | bytes 524292 | tf_op jit(solution)/shard_map/reduce-window
  27.7 0.1 slice.10
  27.8 0.1 copy.75
  28.0 0.1 copy.76
  28.1 0.1 broadcast_add_fusion
  28.3 0.1 fusion.33
  28.3 0.1 reduce_sum.35
  28.4 0.6 broadcast_multiply_fusion
  29.1 1.2 fusion.30
  30.3 0.7 reshape.92
  31.0 8.4 %all-to-all-start = ((bf16[32,2,24]{2,1,0:T(2,128)(2,1)}), bf16[32,2,24]{2,1,0:T(2,128)(2,1)S(1)}, u32[]{:S(2)}, u32[]{:S(2)}) async-start(bf16[32,2,24]{2,1,0:T(2,128)(2,1)} %reshape.92), calls=%async_computation | async-start | bytes 32768 | tf_op jit(solution)/shard_map/all_to_all | solution.py:42
  39.4 3.1 fusion.15
  42.5 0.0 all-gather.5.cloned.1.call-done
  42.6 7.5 %convolution_convert_fusion = bf16[1536,4096]{1,0:T(8,128)(2,1)} fusion(bf16[128,1536]{1,0:T(8,128)(2,1)S(1)} %fusion.15, bf16[128,4096]{1,0:T(8,128)(2,1)} %all-gather.5.cloned.1.call-done), kind=kOutput, calls=%fused_computation.2 | convolution fusion | flops 1616904192 | bytes 14024704 | tf_op jit(solution)/shard_map/tr,td->rd/dot_general | solution.py:30
  50.1 0.0 all-to-all-done
  50.1 7.5 %all-to-all-start.2 = ((bf16[32,2,24,4096]{3,2,1,0:T(8,128)(2,1)}), bf16[32,2,24,4096]{3,2,1,0:T(8,128)(2,1)}, u32[]{:S(2)}, u32[]{:S(2)}) async-start(bf16[32,2,24,4096]{3,2,1,0:T(8,128)(2,1)} %bitcast.101), calls=%async_computation.2 | async-start | bytes 25165824 | tf_op jit(solution)/shard_map/all_to_all | solution.py:40
  57.6 0.0 all-gather.3.cloned.1.call-start
  57.7 0.7 all-gather.3.cloned.1.call-update
  58.4 27.1 %all-gather.3.cloned.1.call-done = bf16[128,4096]{1,0:T(8,128)(2,1)} async-done(((bf16[128,1024]{1,0:T(8,128)(2,1)}), bf16[128,4096]{1,0:T(8,128)(2,1)}) %all-gather.3.cloned.1.call-update) | async-done | bytes 1048592 | tf_op jit(solution)/shard_map/all_gather | solution.py:37
  85.5 7.6 %convolution_convert_fusion.1 = bf16[1536,4096]{1,0:T(8,128)(2,1)} fusion(bf16[128,1536]{1,0:T(8,128)(2,1)S(1)} %fusion.15, bf16[128,4096]{1,0:T(8,128)(2,1)} %all-gather.3.cloned.1.call-done), kind=kOutput, calls=%fused_computation.3 | convolution fusion | flops 1616904192 | bytes 14024704 | tf_op jit(solution)/shard_map/tr,td->rd/dot_general | solution.py:30
  93.1 140.7 %all-to-all-done.2 = bf16[32,2,24,4096]{3,2,1,0:T(8,128)(2,1)} async-done(((bf16[32,2,24,4096]{3,2,1,0:T(8,128)(2,1)}), bf16[32,2,24,4096]{3,2,1,0:T(8,128)(2,1)}, u32[]{:S(2)}, u32[]{:S(2)}) %all-to-all-start.2) | async-done | bytes 12582944 | tf_op jit(solution)/shard_map/all_to_all | solution.py:40
  233.7 28.2 %all-to-all-start.1 = ((bf16[32,2,24,4096]{3,2,1,0:T(8,128)(2,1)}), bf16[32,2,24,4096]{3,2,1,0:T(8,128)(2,1)}, u32[]{:S(2)}, u32[]{:S(2)}) async-start(bf16[32,2,24,4096]{3,2,1,0:T(8,128)(2,1)} %bitcast.102), calls=%async_computation.1 | async-start | bytes 25165824 | tf_op jit(solution)/shard_map/all_to_all | solution.py:41
  261.9 0.2 reduce-scatter.2.cloned.1.call-start
  262.2 0.1 copy.77
  262.3 0.1 copy.78
  262.3 11.1 %fusion.3 = f32[2,32,24,384]{3,2,1,0:T(8,128)S(1)} fusion(bf16[32,2,24,4096]{3,2,1,0:T(8,128)(2,1)} %all-to-all-done.2, bf16[2,4096,384]{2,1,0:T(8,128)(2,1)} %param.11), kind=kOutput, calls=%fused_computation.7 | convolution fusion | flops 4831838208 | bytes 21233664 | tf_op jit(solution)/shard_map/secd,edf->secf/dot_general | solution.py:44
  273.4 164.6 %all-to-all-done.1 = bf16[32,2,24,4096]{3,2,1,0:T(8,128)(2,1)} async-done(((bf16[32,2,24,4096]{3,2,1,0:T(8,128)(2,1)}), bf16[32,2,24,4096]{3,2,1,0:T(8,128)(2,1)}, u32[]{:S(2)}, u32[]{:S(2)}) %all-to-all-start.1) | async-done | bytes 12582944 | tf_op jit(solution)/shard_map/all_to_all | solution.py:41
  438.1 11.1 %fusion.1 = f32[2,32,24,384]{3,2,1,0:T(8,128)S(1)} fusion(bf16[32,2,24,4096]{3,2,1,0:T(8,128)(2,1)} %all-to-all-done.1, bf16[2,384,4096]{2,1,0:T(8,128)(2,1)} %param.13), kind=kOutput, calls=%fused_computation.5 | convolution fusion | flops 4831838208 | bytes 21233664 | tf_op jit(solution)/shard_map/secd,efd->secf/dot_general | solution.py:46
  449.2 0.0 copy-start
  449.2 13.6 %fusion.25 = (f32[32,2,24]{2,0,1:T(8,128)S(1)}, f32[2,32,24,384]{3,2,1,0:T(8,128)}) fusion(f32[2,32,24,384]{3,2,1,0:T(8,128)S(1)} %fusion.1, f32[2,32,24,384]{3,2,1,0:T(8,128)S(1)} %fusion.3, bf16[2,4096,384]{2,1,0:T(8,128)(2,1)} %param.12, bf16[32,2,24,4096]{3,2,1,0:T(8,128)(2,1)} %all-to-all-done.2), kind=kOutput, calls=%fused_computation.35 | convolution fusion | flops 4835965440 | bytes 25958400 | tf_op jit(solution)/shard_map/secd,edf->secf/dot_general | solution.py:45
  462.8 0.0 copy-done
  462.8 16.0 %fusion.7 = f32[2,32,24,4096]{3,2,1,0:T(8,128)} fusion(bf16[2,4096,384]{2,1,0:T(8,128)(2,1)} %param.11, f32[2,32,24,384]{3,2,1,0:T(8,128)S(1)} %fusion.3, f32[2,32,24,384]{3,2,1,0:T(8,128)} %get-tuple-element.17, f32[2,32,24,384]{3,2,1,0:T(8,128)} %copy-done, f32[32,2,24]{2,0,1:T(8,128)S(1)} %copy.78), kind=kOutput, calls=%fused_computation.11 | convolution fusion | flops 4838326272 | bytes 38541312 | tf_op jit(solution)/shard_map/secf,edf->secd/dot_general | solution.py:57
  478.8 19.0 %fusion = bf16[32,2,24,4096]{3,2,0,1:T(8,128)(2,1)} fusion(f32[2,32,24,4096]{3,2,1,0:T(8,128)} %fusion.7, bf16[2,4096,384]{2,1,0:T(8,128)(2,1)} %param.12, f32[2,32,24,384]{3,2,1,0:T(8,128)} %copy-done, f32[32,2,24]{2,0,1:T(8,128)S(1)} %copy.78, f32[2,32,24,384]{3,2,1,0:T(8,128)S(1)} %fusion.3), kind=kOutput, calls=%fused_computation.4 | convolution fusion | flops 4848549888 | bytes 48764928 | tf_op jit(solution)/shard_map/secf,edf->secd/dot_general | solution.py:58
  497.8 0.0 reduce-scatter.2.cloned.1.call-update
  497.8 0.1 copy.83
  497.8 17.0 %psum.7 = bf16[32,2,24]{0,2,1:T(8,128)(2,1)S(1)} all-reduce(f32[32,2,24]{0,2,1:T(8,128)S(1)} %copy.83), channel_id=1, replica_groups=mesh['ctx'=32,'tp'=4] {'tp'}, use_global_device_ids=true, to_apply=%region_6.7 | all-reduce | flops 1536 | bytes 9216 | tf_op jit(solution)/shard_map/psum | solution.py:51
  514.9 0.7 copy.84
  515.6 28.3 %all-to-all-start.4 = ((bf16[32,2,24]{2,1,0:T(2,128)(2,1)}), bf16[32,2,24]{2,1,0:T(2,128)(2,1)S(1)}, u32[]{:S(2)}, u32[]{:S(2)}) async-start(bf16[32,2,24]{2,1,0:T(2,128)(2,1)} %copy.84), calls=%async_computation.5 | async-start | bytes 32768 | tf_op jit(solution)/shard_map/all_to_all | solution.py:66
  543.9 90.7 %reduce-scatter.2.cloned.1.call-done = bf16[32,2,24,1024]{3,2,0,1:T(8,128)(2,1)} async-done(((bf16[32,2,24,4096]{3,2,0,1:T(8,128)(2,1)}), bf16[32,2,24,1024]{3,2,0,1:T(8,128)(2,1)}) %reduce-scatter.2.cloned.1.call-update) | async-done | bytes 3145744 | tf_op jit(solution)/shard_map/reduce_scatter | solution.py:61
  634.5 4.0 copy.82
  638.5 0.0 all-to-all-done.4
  638.5 0.0 copy-start.1
  638.5 0.6 copy-done.1
  639.1 7.3 %all-to-all-start.3 = ((bf16[32,2,24,1024]{3,2,1,0:T(8,128)(2,1)}), bf16[32,2,24,1024]{3,2,1,0:T(8,128)(2,1)S(1)}, u32[]{:S(2)}, u32[]{:S(2)}) async-start(bf16[32,2,24,1024]{3,2,1,0:T(8,128)(2,1)} %copy.82), calls=%async_computation.4 | async-start | bytes 6291456 | tf_op jit(solution)/shard_map/all_to_all | solution.py:65
  646.4 0.9 mul.67
  647.3 0.8 reshape.96
  648.2 6.8 gather_fusion
  655.0 0.7 reshape.97
  655.7 1.4 copy.85
  657.1 29.2 %all-to-all-done.3 = bf16[32,2,24,1024]{3,2,1,0:T(8,128)(2,1)S(1)} async-done(((bf16[32,2,24,1024]{3,2,1,0:T(8,128)(2,1)}), bf16[32,2,24,1024]{3,2,1,0:T(8,128)(2,1)S(1)}, u32[]{:S(2)}, u32[]{:S(2)}) %all-to-all-start.3) | async-done | bytes 3145760 | tf_op jit(solution)/shard_map/all_to_all | solution.py:65
  686.3 1.3 convolution_convert_fusion.2
  (5 shorter events, 0.1 us)
Async XLA Ops:
  7.2 35.4 %all-gather.5.cloned.1.call-start = ((), (), s32[]{:S(2)}) async-start(), calls=%async_computation.7 | async-start | bytes 1310720 | tf_op jit(solution)/shard_map/all_gather | solution.py:36
  31.0 19.1 %all-to-all-start = ((bf16[32,2,24]{2,1,0:T(2,128)(2,1)}), bf16[32,2,24]{2,1,0:T(2,128)(2,1)S(1)}, u32[]{:S(2)}, u32[]{:S(2)}) async-start(bf16[32,2,24]{2,1,0:T(2,128)(2,1)} %reshape.92), calls=%async_computation | async-start | bytes 32768 | tf_op jit(solution)/shard_map/all_to_all | solution.py:42
  50.1 183.6 %all-to-all-start.2 = ((bf16[32,2,24,4096]{3,2,1,0:T(8,128)(2,1)}), bf16[32,2,24,4096]{3,2,1,0:T(8,128)(2,1)}, u32[]{:S(2)}, u32[]{:S(2)}) async-start(bf16[32,2,24,4096]{3,2,1,0:T(8,128)(2,1)} %bitcast.101), calls=%async_computation.2 | async-start | bytes 25165824 | tf_op jit(solution)/shard_map/all_to_all | solution.py:40
  57.6 27.8 %all-gather.3.cloned.1.call-start = ((), (), s32[]{:S(2)}) async-start(), calls=%async_computation.6 | async-start | bytes 1310720 | tf_op jit(solution)/shard_map/all_gather | solution.py:37
  233.7 204.3 %all-to-all-start.1 = ((bf16[32,2,24,4096]{3,2,1,0:T(8,128)(2,1)}), bf16[32,2,24,4096]{3,2,1,0:T(8,128)(2,1)}, u32[]{:S(2)}, u32[]{:S(2)}) async-start(bf16[32,2,24,4096]{3,2,1,0:T(8,128)(2,1)} %bitcast.102), calls=%async_computation.1 | async-start | bytes 25165824 | tf_op jit(solution)/shard_map/all_to_all | solution.py:41
  261.9 372.6 %reduce-scatter.2.cloned.1.call-start = ((), (), s32[]{:S(2)}) async-start(), calls=%async_computation.8 | async-start | bytes 15728640 | tf_op jit(solution)/shard_map/reduce_scatter | solution.py:61
  449.2 13.7 %copy-start = (f32[2,32,24,384]{3,2,1,0:T(8,128)}, f32[2,32,24,384]{3,2,1,0:T(8,128)S(1)}, u32[]{:S(2)}) copy-start(f32[2,32,24,384]{3,2,1,0:T(8,128)S(1)} %fusion.1) | copy-start | bytes 7077892
  515.6 122.9 %all-to-all-start.4 = ((bf16[32,2,24]{2,1,0:T(2,128)(2,1)}), bf16[32,2,24]{2,1,0:T(2,128)(2,1)S(1)}, u32[]{:S(2)}, u32[]{:S(2)}) async-start(bf16[32,2,24]{2,1,0:T(2,128)(2,1)} %copy.84), calls=%async_computation.5 | async-start | bytes 32768 | tf_op jit(solution)/shard_map/all_to_all | solution.py:66
  638.5 0.6 copy-start.1
  639.1 47.2 %all-to-all-start.3 = ((bf16[32,2,24,1024]{3,2,1,0:T(8,128)(2,1)}), bf16[32,2,24,1024]{3,2,1,0:T(8,128)(2,1)S(1)}, u32[]{:S(2)}, u32[]{:S(2)}) async-start(bf16[32,2,24,1024]{3,2,1,0:T(8,128)(2,1)} %copy.82), calls=%async_computation.4 | async-start | bytes 6291456 | tf_op jit(solution)/shard_map/all_to_all | solution.py:65
Sparse Core Ops, SparseCore 0:
  9.7 26.3 all-gather.4
  60.1 25.2 all-gather.2
  497.9 136.5 reduce-scatter.1
where the time goes:
time: 696 us; the launch traced here: 694 us
  waiting for transfers between devices  454 us (65%)
  matrix products  88.4 us (13%)
  starting transfers between devices  79.9 us (11%)
  other arithmetic  22 us (3%)
  local copies, waits for them, and re-layouts  19.1 us (3%)
  blocking collectives  17 us (2%)
  between operations  13.9 us (2%)
    all_to_all x1, waiting for transfers between devices, on_device(): lax.all_to_all(arrange(full_grads), 'ctx', split_axis=0, concat_axis=0, t...  165 us
    all_to_all x1, waiting for transfers between devices, on_device(): lax.all_to_all(arrange(full_tokens), 'ctx', split_axis=0, concat_axis=0,...  141 us
    reduce_scatter x1, waiting for transfers between devices, on_device(): lax.psum_scatter(row_part.astype(jnp.bfloat16), 'tp', scatter_dimension=3...  90.7 us
    all_to_all x1, waiting for transfers between devices, on_device(): lax.all_to_all(row_grads, 'ctx', split_axis=0, concat_axis=0, tiled=True)  29.2 us
    all_to_all x1, starting transfers between devices, on_device(): lax.all_to_all(prob_total.astype(jnp.bfloat16), 'ctx', split_axis=0, conc...  28.3 us
    all_to_all x1, starting transfers between devices, on_device(): lax.all_to_all(arrange(full_grads), 'ctx', split_axis=0, concat_axis=0, t...  28.2 us
    all_gather x1, waiting for transfers between devices, on_device(): lax.all_gather(out_grad, 'tp', axis=1, tiled=True)  27.1 us
    dot_general x1, matrix products, on_device(): jnp.einsum('secf,edf->secd', up_grad, w_up, preferred_element_type=jnp.fl...  19 us
  transfers between devices with their start and end apart: 8, of which 5 were waited for; matrix products, arithmetic and copies ran while one was open for 10% of the time, Pallas kernels for 0%

commit v1 on v0

v1 whole, which is shorter than its diff:
```python
import functools
import jax
import jax.numpy as jnp
from jax import lax
from jax.experimental import pallas as pl
from jax.experimental.pallas import tpu as pltpu
from jax.sharding import PartitionSpec as P

MESH = pl.DeviceIdType.MESH
ORDERS = (("x", "y", "z"), ("y", "z", "x"), ("z", "x", "y"))
SPLITS = (((0, 40), (40, 40), (80, 48)), ((0, 48), (48, 40), (88, 40)))


def my_place():
    ctx = lax.axis_index("ctx")
    return {"x": lax.axis_index("tp"), "y": ctx // 8, "z": (ctx // 2) % 4}, ctx % 2


def device_of(pos, core):
    return ((pos["y"] * 4 + pos["z"]) * 2 + core, pos["x"])


def shifted(pos, axis, by):
    other = dict(pos)
    other[axis] = (pos[axis] + by) % 4
    return other


def entry_barrier(pos, core):
    barrier = pltpu.get_barrier_semaphore()
    for axis in "xyz":
        for by in (1, 3):
            pl.semaphore_signal(barrier, inc=1, device_id=device_of(shifted(pos, axis, by), core), device_id_type=MESH)
    pl.semaphore_signal(barrier, inc=1, device_id=device_of(pos, 1 - core), device_id_type=MESH)
    pl.semaphore_wait(barrier, 7)


def gather_kernel(tok_ref, dy_ref, gx_ref, gy_ref, send, recv, local):
    pos, core = my_place()
    entry_barrier(pos, core)
    width = tok_ref.shape[1]
    own = []
    for t, (src, dst) in enumerate(((tok_ref, gx_ref), (dy_ref, gy_ref))):
        copy = pltpu.make_async_copy(src, dst.at[pos["y"], pos["z"], core, pos["x"]], local.at[t])
        copy.start()
        own.append(copy)
    started = []

    def program(t, color):
        src, dst = ((tok_ref, gx_ref), (dy_ref, gy_ref))[t]
        a, b, c = ORDERS[color]
        r0, rn = SPLITS[t][color]
        rows = pl.ds(r0, rn)

        def slot(at, whole, part=None):
            index = {k: (slice(None) if k in whole else at[k]) for k in "xyz"}
            some = rows
            if part is not None and whole:
                index[a] = pl.ds(2 * part, 2)
            elif part is not None:
                some = pl.ds(r0, 24) if part == 0 else pl.ds(r0 + 24, rn - 24)
            return dst.at[index["y"], index["z"], core, index["x"], some]

        def go(i, source, target, device):
            copy = pltpu.make_async_remote_copy(
                src_ref=source, dst_ref=target, send_sem=send.at[t, color, i],
                recv_sem=recv.at[t, color, i], device_id=device, device_id_type=MESH)
            copy.start()
            started.append(copy)
            return copy

        def block_out(i, at, whole, axis, source=None):
            here = slot(at, whole)
            from_ref = here if source is None else source
            return (go(i, from_ref, here, device_of(shifted(pos, axis, 1), core)),
                    go(i + 1, from_ref, here, device_of(shifted(pos, axis, 3), core)))

        def relay(i, at, whole, axis, pair):
            pair[0].wait_recv()
            piece = slot(shifted(at, axis, 3), whole, 0)
            one = go(i + 2, piece, piece, device_of(shifted(pos, axis, 1), core))
            pair[1].wait_recv()
            piece = slot(shifted(at, axis, 1), whole, 1)
            two = go(i + 3, piece, piece, device_of(shifted(pos, axis, 3), core))
            return one, two

        sib_count = [0]
        sibs = []

        def sibling(at):
            piece = slot(at, (a,))
            sibs.append(go(24 + sib_count[0], piece, piece, device_of(pos, 1 - core)))
            sib_count[0] += 1

        pair = block_out(0, pos, (), a, src.at[rows, :])
        yield
        far = relay(0, pos, (), a, pair)
        yield
        for f in far:
            f.wait_recv()
        if own[t] is not None:
            own[t].wait()
            own[t] = None
        pair = block_out(4, pos, (a,), b)
        lasts = [(8, pos, block_out(8, pos, (a,), c))]
        sibling(pos)
        yield
        far = relay(4, pos, (a,), b, pair)
        for n, by in ((12, 3), (16, 1)):
            at = shifted(pos, b, by)
            lasts.append((n, at, block_out(n, at, (a,), c)))
            sibling(at)
        yield
        for f in far:
            f.wait_recv()
        at = shifted(pos, b, 2)
        lasts.append((20, at, block_out(20, at, (a,), c)))
        sibling(at)
        fars = []
        for n, at, pair in lasts:
            yield
            fars.append((at, relay(n, at, (a,), c, pair)))
            sibling(shifted(at, c, 3))
            sibling(shifted(at, c, 1))
            if len(fars) > 1:
                at2, far = fars[-2]
                for f in far:
                    f.wait_recv()
                sibling(shifted(at2, c, 2))
        yield
        at2, far = fars[-1]
        for f in far:
            f.wait_recv()
        sibling(shifted(at2, c, 2))
        yield
        for s in sibs:
            s.wait_recv()

    LAG = 4
    running = [(0, program(0, col)) for col in range(3)] + [(LAG, program(1, col)) for col in range(3)]
    tick = 0
    live = list(running)
    while live:
        still = []
        for first, prog in live:
            if tick < first:
                still.append((first, prog))
                continue
            try:
                next(prog)
                still.append((first, prog))
            except StopIteration:
                pass
        live = still
        tick += 1
    for s in started:
        s.wait_send()


def gather_all(tokens, out_grad):
    rows, width = tokens.shape
    shape = jax.ShapeDtypeStruct((4, 4, 2, 4, rows, width), tokens.dtype)
    return pl.pallas_call(
        gather_kernel,
        out_shape=(shape, shape),
        in_specs=[pl.BlockSpec(memory_space=pltpu.VMEM)] * 2,
        out_specs=[pl.BlockSpec(memory_space=pl.ANY)] * 2,
        scratch_shapes=[
            pltpu.SemaphoreType.DMA((2, 3, 40)),
            pltpu.SemaphoreType.DMA((2, 3, 40)),
            pltpu.SemaphoreType.DMA((2,)),
        ],
        compiler_params=pltpu.CompilerParams(collective_id=0, has_side_effects=True),
    )(tokens, out_grad)

CAPS = 24


def pair_selectors(ids, probs, first):
    groups, top, toks = ids.shape
    before = (lax.broadcasted_iota(jnp.int32, (toks, toks), 0) < lax.broadcasted_iota(jnp.int32, (toks, toks), 1)).astype(jnp.bfloat16)
    out = []
    for e in range(2):
        masks, hits, slots, weights = [], [], [], []
        for g in range(2):
            mask = (ids[g] == first + e).astype(jnp.float32)
            hit = jnp.sum(mask, axis=0, keepdims=True)
            slot = jnp.dot(jnp.broadcast_to(hit, (8, toks)).astype(jnp.bfloat16), before, preferred_element_type=jnp.float32)[0:1]
            masks.append(mask)
            hits.append(hit)
            slots.append(slot + float(CAPS * g))
            weights.append(jnp.sum(mask * probs[g], axis=0, keepdims=True))
        hit = jnp.concatenate(hits, axis=1)
        slot = jnp.concatenate(slots, axis=1)
        weight = jnp.concatenate(weights, axis=1)
        row = lax.broadcasted_iota(jnp.int32, (2 * CAPS, 2 * toks), 0)
        sel = jnp.where((row == slot.astype(jnp.int32)) & (hit > 0.5), 1.0, 0.0)
        out.append((sel, weight, masks))
    return out


def expert_kernel(ids_ref, probs_ref, x_ref, dy_ref, wg_ref, wu_ref, wd_ref, out_ref, pg_ref,
                  xr, dr, rp, pw, pr, *, sets, per_set):
    step = pl.program_id(0)
    first = lax.axis_index("ctx") * 2
    steps = sets * per_set
    width = x_ref.shape[3]
    quarters = x_ref.shape[1]
    toks = x_ref.shape[2]

    @pl.when(step >= per_set)
    def _():
        i = step - per_set
        at = pl.multiple_of(lax.rem(i, per_set) * 2 * CAPS, 16)
        pair = pl.ds(2 * i, 2)
        chosen = pair_selectors(ids_ref[pair], probs_ref[pair], first)
        both = jnp.concatenate([c[0] for c in chosen], axis=0).astype(jnp.bfloat16)
        for q in range(quarters):
            cols = pl.ds(q * width, width)
            rows = jnp.concatenate([rp[e, pl.ds(at, 2 * CAPS), cols] for e in range(2)], axis=0)
            dense = lax.dot_general(both, rows, (((0,), (0,)), ((), ())), preferred_element_type=jnp.float32)
            dense = dense.astype(jnp.bfloat16)
            for g in range(2):
                out_ref[g, q] = dense[g * toks:(g + 1) * toks]
        total = [0.0, 0.0]
        for e in range(2):
            sel, _w, masks = chosen[e]
            value = jnp.sum(sel * pr[e, pl.ds(at, 2 * CAPS), 0:1], axis=0, keepdims=True)
            for g in range(2):
                total[g] = total[g] + masks[g] * value[:, g * toks:(g + 1) * toks]
        for g in range(2):
            pg_ref[g] = total[g]

    @pl.when(step < steps)
    def _():
        at = pl.multiple_of(lax.rem(step, per_set) * 2 * CAPS, 16)
        pair = pl.ds(2 * step, 2)
        chosen = pair_selectors(ids_ref[pair], probs_ref[pair], first)
        both = jnp.concatenate([c[0] for c in chosen], axis=0).astype(jnp.bfloat16)
        for src, dst in ((x_ref, xr), (dy_ref, dr)):
            for q in range(quarters):
                two = src[:, q].reshape(2 * toks, width)
                rows = jnp.dot(both, two, preferred_element_type=jnp.float32).astype(jnp.bfloat16)
                for e in range(2):
                    dst[e, pl.ds(at, 2 * CAPS), pl.ds(q * width, width)] = rows[e * 2 * CAPS:(e + 1) * 2 * CAPS]
        for e in range(2):
            sel, weight, _m = chosen[e]
            col = jnp.sum(sel * weight, axis=1, keepdims=True)
            pw[e, pl.ds(at, 2 * CAPS), :] = jnp.broadcast_to(col, (2 * CAPS, 128))

    @pl.when((step < steps) & (lax.rem(step, per_set) == per_set - 1))
    def _():
        for e in range(2):
            gate = jnp.dot(xr[e], wg_ref[e], preferred_element_type=jnp.float32)
            up = jnp.dot(xr[e], wu_ref[e], preferred_element_type=jnp.float32)
            back = lax.dot_general(dr[e], wd_ref[e], (((1,), (1,)), ((), ())), preferred_element_type=jnp.float32)
            sig = jax.nn.sigmoid(gate)
            gated = gate * sig
            pr[e] = jnp.broadcast_to(jnp.sum(gated * up * back, axis=1, keepdims=True), pr.shape[1:])
            scaled = pw[e, :, 0:1] * back
            gg = (scaled * up * sig * (1.0 + gate * (1.0 - sig))).astype(jnp.bfloat16)
            ug = (scaled * gated).astype(jnp.bfloat16)
            dims = (((1,), (1,)), ((), ()))
            depth = wg_ref.shape[1]
            block = 1024
            for d in range(depth // block):
                cols = pl.ds(d * block, block)
                part = lax.dot_general(gg, wg_ref[e, cols, :], dims, preferred_element_type=jnp.float32)
                part = part + lax.dot_general(ug, wu_ref[e, cols, :], dims, preferred_element_type=jnp.float32)
                rp[e, :, cols] = part.astype(jnp.bfloat16)


def expert_pass(ids, probs, gx, gy, wg, wu, wd):
    groups, quarters, toks, width = gx.shape
    depth, ff = wg.shape[1:]
    per_set = 4
    sets = groups // 2 // per_set
    steps = sets * per_set
    rows = per_set * 2 * CAPS
    one = pl.Buffered(1)
    zero3 = lambda i: (0, 0, 0)
    return pl.pallas_call(
        functools.partial(expert_kernel, sets=sets, per_set=per_set),
        grid=(steps + per_set,),
        out_shape=(jax.ShapeDtypeStruct(gx.shape, jnp.bfloat16), jax.ShapeDtypeStruct((groups,) + ids.shape[1:], jnp.float32)),
        in_specs=[
            pl.BlockSpec(ids.shape, zero3),
            pl.BlockSpec(probs.shape, zero3),
            pl.BlockSpec((2, quarters, toks, width), lambda i: (jnp.minimum(i, steps - 1), 0, 0, 0)),
            pl.BlockSpec((2, quarters, toks, width), lambda i: (jnp.minimum(i, steps - 1), 0, 0, 0)),
            pl.BlockSpec(wg.shape, zero3, pipeline_mode=one),
            pl.BlockSpec(wu.shape, zero3, pipeline_mode=one),
            pl.BlockSpec(wd.shape, zero3, pipeline_mode=one),
        ],
        out_specs=[
            pl.BlockSpec((2, quarters, toks, width), lambda i: (jnp.maximum(i - per_set, 0), 0, 0, 0)),
            pl.BlockSpec((2,) + ids.shape[1:], lambda i: (jnp.maximum(i - per_set, 0), 0, 0)),
        ],
        scratch_shapes=[
            pltpu.VMEM((2, rows, depth), jnp.bfloat16),
            pltpu.VMEM((2, rows, depth), jnp.bfloat16),
            pltpu.VMEM((2, rows, depth), jnp.bfloat16),
            pltpu.VMEM((2, rows, 128), jnp.float32),
            pltpu.VMEM((2, rows, 128), jnp.float32),
        ],
        compiler_params=pltpu.CompilerParams(vmem_limit_bytes=60 * 1024 * 1024),
    )(ids, probs, gx, gy, wg, wu, wd)

PARTS = ((0, 48), (48, 48), (96, 32))


def scatter_kernel(p_ref, out_ref, *scratch):
    accs, sibs, fulls, parts, lone_full, lone_part = (scratch[3 * i:3 * i + 3] for i in range(6))
    send, recv, local = scratch[18:]
    pos, core = my_place()
    entry_barrier(pos, core)
    width = out_ref.shape[1]
    half = width // 2
    cuts = (pl.ds(0, half), pl.ds(half, half))
    started = []

    def go(color, i, source, target, device):
        copy = pltpu.make_async_remote_copy(
            src_ref=source, dst_ref=target, send_sem=send.at[color, i],
            recv_sem=recv.at[color, i], device_id=device, device_id_type=MESH)
        copy.start()
        started.append(copy)
        return copy

    def program(color):
        a, b, c = ORDERS[color]
        rows = pl.ds(*PARTS[color])
        acc, sib = accs[color], sibs[color]

        def where(at, whole):
            index = {k: (slice(None) if k in whole else at[k]) for k in "xyz"}
            return index["y"], index["z"], index["x"]

        def line(at, part=None):
            index = dict(zip("yzx", where(at, (a,))))
            if part is not None:
                index[a] = pl.ds(2 * part, 2)
            return acc.at[index["y"], index["z"], index["x"]]

        def add_line(at, part, other):
            low, high = (0, 4) if part is None else (2 * part, 2 * part + 2)

            def body(i, carry):
                mine = dict(at)
                mine[a] = i
                spot = where(mine, ())
                acc[spot] = acc[spot] + other(i - low)
                return carry
            lax.fori_loop(low, high, body, 0)

        loads = {}
        order = (2, 1, 3, 0)
        count = 0
        for j in order:
            for k in order:
                at = shifted(shifted(pos, b, j), c, k)
                y, z, x = where(at, (a,))
                load = pltpu.make_async_copy(p_ref.at[y, z, core, x, rows], line(at), local.at[color, count])
                load.start()
                push = go(color, 24 + count, p_ref.at[y, z, 1 - core, x, rows], sib.at[y, z, x], device_of(pos, 1 - core))
                loads[j, k] = (at, load, push)
                count += 1
            yield

        def merge(j, k):
            at, load, push = loads[j, k]
            load.wait()
            push.wait_recv()

            def other(i):
                mine = dict(at)
                mine[a] = i
                return sib[where(mine, ())]
            add_line(at, None, other)

        def first(n, axis, unit):
            return (go(color, n * 4, unit(2, 0), parts[color].at[n, 0], device_of(shifted(pos, axis, 1), core)),
                    go(color, n * 4 + 1, unit(2, 1), parts[color].at[n, 1], device_of(shifted(pos, axis, 3), core)))

        def second(n, axis, unit, add, halves):
            sent = []
            for side, by in ((0, 1), (1, 3)):
                halves[side].wait_recv()
                add(by, side, lambda i, side=side: parts[color][n, side, i])
                sent.append(go(color, n * 4 + 2 + side, unit(by, None), fulls[color].at[n, side],
                               device_of(shifted(pos, axis, by), core)))
            return sent

        def third(n, add, sent):
            for side in range(2):
                sent[side].wait_recv()
                add(0, None, lambda i, side=side: fulls[color][n, side, i])

        def last_unit(j):
            return (lambda k, cols: line(shifted(shifted(pos, b, j), c, k), cols),
                    lambda k, cols, other: add_line(shifted(shifted(pos, b, j), c, k), cols, other))

        halves, sents = {}, {}

        def stage_a(n):
            merge(order[n], 2)
            halves[n] = first(n, c, last_unit(order[n])[0])

        def stage_b(n):
            merge(order[n], 1)
            merge(order[n], 3)
            unit, add = last_unit(order[n])
            sents[n] = second(n, c, unit, add, halves[n])

        def stage_c(n):
            merge(order[n], 0)
            third(n, last_unit(order[n])[1], sents[n])

        mid_unit = lambda k, cols: line(shifted(pos, b, k), cols)
        mid_add = lambda k, cols, other: add_line(shifted(pos, b, k), cols, other)
        stage_a(0)
        yield
        stage_a(1)
        yield
        stage_b(0)
        yield
        stage_a(2)
        yield
        stage_b(1)
        yield
        stage_c(0)
        mid_halves = first(4, b, mid_unit)
        yield
        stage_a(3)
        yield
        stage_b(2)
        yield
        stage_c(1)
        yield
        stage_b(3)
        yield
        stage_c(2)
        mid_sent = second(4, b, mid_unit, mid_add, mid_halves)
        yield
        stage_c(3)
        third(4, mid_add, mid_sent)
        yield

        def one(at, cols=slice(None)):
            return acc.at[(*where(at, ()), slice(None), cols)]

        def add_one(by, cols, other):
            spot = (*where(shifted(pos, a, by), ()), slice(None), cols)
            acc[spot] = acc[spot] + other

        tail = [go(color, 20, one(shifted(pos, a, 2), cuts[0]), lone_part[color].at[0], device_of(shifted(pos, a, 1), core)),
                go(color, 21, one(shifted(pos, a, 2), cuts[1]), lone_part[color].at[1], device_of(shifted(pos, a, 3), core))]
        yield
        sent = []
        for side, by in ((0, 1), (1, 3)):
            tail[side].wait_recv()
            add_one(by, cuts[side], lone_part[color][side])
            sent.append(go(color, 22 + side, one(shifted(pos, a, by)), lone_full[color].at[side], device_of(shifted(pos, a, by), core)))
        yield
        for side in range(2):
            sent[side].wait_recv()
            add_one(0, slice(None), lone_full[color][side])
        out_ref[rows, :] = acc[where(pos, ())]

    live = [program(color) for color in range(3)]
    while live:
        still = []
        for prog in live:
            try:
                next(prog)
                still.append(prog)
            except StopIteration:
                pass
        live = still
    for s in started:
        s.wait_send()


def scatter_all(dense):
    rows, width = dense.shape[-2:]
    half = width // 2
    bf = jnp.bfloat16
    scratch = []
    for make in (
        lambda n: (4, 4, 4, n, width),
        lambda n: (4, 4, 4, n, width),
        lambda n: (5, 2, 4, n, width),
        lambda n: (5, 2, 2, n, width),
        lambda n: (2, n, width),
        lambda n: (2, n, half),
    ):
        scratch += [pltpu.VMEM(make(n), bf) for _, n in PARTS]
    return pl.pallas_call(
        scatter_kernel,
        out_shape=jax.ShapeDtypeStruct((rows, width), bf),
        in_specs=[pl.BlockSpec(memory_space=pl.ANY)],
        out_specs=pl.BlockSpec(memory_space=pltpu.VMEM),
        scratch_shapes=scratch + [
            pltpu.SemaphoreType.DMA((3, 40)),
            pltpu.SemaphoreType.DMA((3, 40)),
            pltpu.SemaphoreType.DMA((3, 16)),
        ],
        compiler_params=pltpu.CompilerParams(collective_id=1, has_side_effects=True, vmem_limit_bytes=62 * 1024 * 1024),
    )(dense)


def on_device(tokens, out_grad, router_probs, expert_ids, w_gate, w_up, w_down):
    toks, width = tokens.shape
    gx, gy = gather_all(tokens, out_grad)
    ids = lax.all_gather(expert_ids.T, "ctx", axis=0)
    probs = lax.all_gather(router_probs.T, "ctx", axis=0).astype(jnp.float32)
    flat = (32, 4, toks, width)
    dense, pg = expert_pass(ids, probs, gx.reshape(flat), gy.reshape(flat), w_gate, w_up, w_down)
    token_grad = scatter_all(dense.reshape(gx.shape))
    pg = lax.psum_scatter(pg, "ctx", scatter_dimension=0, tiled=True)
    pg = lax.psum(pg, "tp")
    return token_grad, pg[0].T.astype(jnp.bfloat16)


def solution(mesh):
    return jax.shard_map(
        on_device,
        mesh=mesh,
        in_specs=(P("ctx", "tp"), P("ctx", "tp"), P("ctx", None), P("ctx", None), P("ctx", None, "tp"), P("ctx", None, "tp"), P("ctx", "tp", None)),
        out_specs=(P("ctx", "tp"), P("ctx", None)),
        check_vma=False,
    )
```

time: 696 us -> 415 us (0.60)
  waiting for transfers between devices: 454 us -> 14.7 us
  Pallas kernels: 0 us -> 318 us
  matrix products: 88.4 us -> 0 us
  starting transfers between devices: 79.9 us -> 0.04 us
  blocking collectives: 17 us -> 62.7 us
  other arithmetic: 22 us -> 0.66 us
  local copies, waits for them, and re-layouts: 19.1 us -> 3.58 us
    all_to_all x5 -> x0, waiting for transfers between devices: 335 us -> none  [the longest x1 165 us: on_device(): lax.all_to_all(arrange(full_grads), 'ctx', split_axis=0, concat_axis=0, t...]
    pallas_call x0 -> x3, Pallas kernels: none -> 318 us  [the longest x1 145 us: gather_all(): pl.pallas_call(gather_kernel, out_shape=(shape, shape), in_specs=[pl.Bloc...]
    reduce_scatter x1 -> x0, waiting for transfers between devices: 90.7 us -> none  [on_device(): lax.psum_scatter(row_part.astype(jnp.bfloat16), 'tp', scatter_dimension=3...]
    dot_general x9 -> x0, matrix products: 88.4 us -> none  [the longest x1 19 us: on_device(): jnp.einsum('secf,edf->secd', up_grad, w_up, preferred_element_type=jnp.fl...]
    all_to_all x5 -> x0, starting transfers between devices: 79.6 us -> none  [the longest x1 28.3 us: on_device(): lax.all_to_all(prob_total.astype(jnp.bfloat16), 'ctx', split_axis=0, conc...]
    all_gather x0 -> x2, blocking collectives: none -> 51.7 us  [the longest x1 25.9 us: on_device(): ids = lax.all_gather(expert_ids.T, 'ctx', axis=0)]
    all_gather x2 -> x0, waiting for transfers between devices: 27.1 us -> none  [the longest x1 27.1 us: on_device(): lax.all_gather(out_grad, 'tp', axis=1, tiled=True)]
    another operation x3 -> x0, other arithmetic: 18.2 us -> none
  transfers between devices with their start and end apart: 8 -> 1, of which waited for: 5 -> 1; matrix products, arithmetic and copies ran while one was open for 10% -> 0% of each run, Pallas kernels for 0% -> 20%
where the time goes in v1:
time: 415 us; the launch traced here: 414 us
  Pallas kernels  318 us (77%)
  blocking collectives  62.7 us (15%)
  waiting for transfers between devices  14.7 us (4%)
  between operations  14.1 us (3%)
    pallas_call x1, Pallas kernels, gather_all(): pl.pallas_call(gather_kernel, out_shape=(shape, shape), in_specs=[pl.Bloc...  145 us
    pallas_call x1, Pallas kernels, expert_pass(): pl.pallas_call(functools.partial(expert_kernel, sets=sets, per_set=per_se...  89.1 us
    pallas_call x1, Pallas kernels, scatter_all(): pl.pallas_call(scatter_kernel, out_shape=jax.ShapeDtypeStruct((rows, widt...  84.3 us
    all_gather x1, blocking collectives, on_device(): ids = lax.all_gather(expert_ids.T, 'ctx', axis=0)  25.9 us
    all_gather x1, blocking collectives, on_device(): probs = lax.all_gather(router_probs.T, 'ctx', axis=0).astype(jnp.float32)  25.7 us
    unnamed x2, waiting for transfers between devices  14.7 us
    psum x1, blocking collectives, on_device(): pg = lax.psum(pg, 'tp')  11 us
  transfers between devices with their start and end apart: 1, of which 1 were waited for; matrix products, arithmetic and copies ran while one was open for 0% of the time, Pallas kernels for 20%

profile of v1, /device:TPU:0, one launch (start us, length us, event | category | flops | bytes accessed | tf_op | source)
XLA Modules:
  0.0 414.2 jit_solution(14244531215487717961)
XLA Ops:
  7.2 0.0 all-reduce.3.cloned.1.call-start
  7.2 25.7 %all-gather.1 = bf16[256,128]{1,0:T(8,128)(2,1)S(1)} all-gather(bf16[8,128]{1,0:T(8,128)(2,1)} %bitcast.20), channel_id=3, replica_groups=mesh['ctx'=32,'tp'=4] {'ctx'}, dimensions={0}, use_global_device_ids=true | all-gather | bytes 67584 | tf_op jit(solution)/shard_map/all_gather | solution.py:516
  33.0 0.7 bitcast_convert_fusion.probs_ref
  33.6 25.9 %all-gather = s32[256,128]{1,0:T(8,128)} all-gather(s32[8,128]{1,0:T(8,128)} %bitcast.19), channel_id=2, replica_groups=mesh['ctx'=32,'tp'=4] {'ctx'}, dimensions={0}, use_global_device_ids=true | all-gather | bytes 135168 | tf_op jit(solution)/shard_map/all_gather | solution.py:515
  59.6 145.0 %shard_map.86 = (bf16[4,4,2,4,128,1024]{5,4,3,2,1,0:T(8,128)(2,1)}, bf16[4,4,2,4,128,1024]{5,4,3,2,1,0:T(8,128)(2,1)}) custom-call(bf16[128,1024]{1,0:T(8,128)(2,1)} %tok_ref.1, bf16[128,1024]{1,0:T(8,128)(2,1)} %dy_ref.1), custom_call_target="tpu_custom_call" | custom-call | tf_op jit(solution)/shard_map/pallas_call | solution.py:163
  204.6 89.1 %shard_map.87 = (bf16[32,4,128,1024]{3,2,1,0:T(8,128)(2,1)}, f32[32,8,128]{2,1,0:T(8,128)}) custom-call(s32[32,8,128]{2,1,0:T(8,128)} %bitcast.18, f32[32,8,128]{2,1,0:T(8,128)} %bitcast_convert_fusion.probs_ref, bf16[32,4,128,1024]{3,2,1,0:T(8,128)(2,1)} %bitcast.16, bf16[32,4,128,1024]{3,2,1,0:T(8,128)(2,1)} %bitcast.17, bf16[2,4096,384]{2,1,0:T(8,128)(2,1)} %wg_ref.1, ...), custom_call_target="tpu_custom_call" | custom-call | tf_op jit(solution)/shard_map/pallas_call | solution.py:282
  293.7 0.0 copy-start
  293.7 0.0 all-reduce.3.cloned.1.call-update
  293.7 84.3 %shard_map.88 = bf16[128,1024]{1,0:T(8,128)(2,1)} custom-call(bf16[4,4,2,4,128,1024]{5,4,3,2,1,0:T(8,128)(2,1)} %bitcast.15), custom_call_target="tpu_custom_call" | custom-call | tf_op jit(solution)/shard_map/pallas_call | solution.py:498
  378.1 0.0 copy-done
  378.1 0.6 dynamic-slice
  378.7 14.7 %all-reduce.3.cloned.1.call-done = f32[32,8,128]{2,1,0:T(8,128)} async-done(((f32[32,8,128]{2,1,0:T(8,128)}), f32[32,8,128]{2,1,0:T(8,128)}) %all-reduce.3.cloned.1.call-update) | async-done | bytes 131088
  393.4 1.3 constant_dynamic-slice_fusion
  394.7 11.0 %psum.7 = bf16[1,8,128]{2,1,0:T(8,128)(2,1)} all-reduce(f32[1,8,128]{2,1,0:T(8,128)S(1)} %constant_dynamic-slice_fusion), channel_id=1, replica_groups=mesh['ctx'=32,'tp'=4] {'tp'}, use_global_device_ids=true, to_apply=%region_1.0 | all-reduce | flops 1024 | bytes 6144 | tf_op jit(solution)/shard_map/psum | solution.py:521
  405.7 1.7 copy.11
Async XLA Ops:
  7.2 386.2 %all-reduce.3.cloned.1.call-start = ((), (), s32[]{:S(2)}) async-start(), calls=%async_computation | async-start | bytes 262144
  293.7 84.4 %copy-start = (u32[128]{0:T(128)S(1)}, u32[128]{0:T(128)}, u32[]{:S(2)}) copy-start(u32[128]{0:T(128)} %constant.5) | copy-start | bytes 1540
Sparse Core Ops, SparseCore 0:
  293.8 99.4 all-reduce.2

commit v2 on v1

--- a/solution.py
+++ b/solution.py
@@ -35,7 +35,7 @@
     pl.semaphore_wait(barrier, 7)
 
 
-def gather_kernel(tok_ref, dy_ref, gx_ref, gy_ref, send, recv, local):
+def gather_kernel(tok_ref, dy_ref, meta_ref, gx_ref, gy_ref, gm_ref, send, recv, msend, mrecv, local):
     pos, core = my_place()
     entry_barrier(pos, core)
     width = tok_ref.shape[1]
@@ -44,7 +44,44 @@
         copy = pltpu.make_async_copy(src, dst.at[pos["y"], pos["z"], core, pos["x"]], local.at[t])
         copy.start()
         own.append(copy)
+    own_meta = pltpu.make_async_copy(meta_ref, gm_ref.at[pos["y"], pos["z"], core], local.at[2])
+    own_meta.start()
     started = []
+
+    def meta_program():
+        def go(i, source, target, device):
+            copy = pltpu.make_async_remote_copy(
+                src_ref=source, dst_ref=target, send_sem=msend.at[i], recv_sem=mrecv.at[i],
+                device_id=device, device_id_type=MESH)
+            copy.start()
+            started.append(copy)
+            return copy
+
+        here = gm_ref.at[pos["y"], pos["z"], core]
+        one = go(0, meta_ref, here, device_of(shifted(pos, "y", 1), core))
+        two = go(1, meta_ref, here, device_of(shifted(pos, "y", 3), core))
+        yield
+        one.wait_recv()
+        back = gm_ref.at[shifted(pos, "y", 3)["y"], pos["z"], core]
+        far = go(2, back, back, device_of(shifted(pos, "y", 1), core))
+        two.wait_recv()
+        yield
+        far.wait_recv()
+        own_meta.wait()
+        here = gm_ref.at[:, pos["z"], core]
+        one = go(3, here, here, device_of(shifted(pos, "z", 1), core))
+        two = go(4, here, here, device_of(shifted(pos, "z", 3), core))
+        yield
+        one.wait_recv()
+        back = gm_ref.at[:, shifted(pos, "z", 3)["z"], core]
+        far = go(5, back, back, device_of(shifted(pos, "z", 1), core))
+        two.wait_recv()
+        yield
+        far.wait_recv()
+        mine = gm_ref.at[:, :, core]
+        last = go(6, mine, mine, device_of(pos, 1 - core))
+        yield
+        last.wait_recv()
 
     def program(t, color):
         src, dst = ((tok_ref, gx_ref), (dy_ref, gy_ref))[t]
@@ -137,7 +174,7 @@
             s.wait_recv()
 
     LAG = 4
-    running = [(0, program(0, col)) for col in range(3)] + [(LAG, program(1, col)) for col in range(3)]
+    running = [(0, meta_program())] + [(0, program(0, col)) for col in range(3)] + [(LAG, program(1, col)) for col in range(3)]
     tick = 0
     live = list(running)
     while live:
@@ -157,27 +194,30 @@
         s.wait_send()
 
 
-def gather_all(tokens, out_grad):
+def gather_all(tokens, out_grad, meta):
     rows, width = tokens.shape
     shape = jax.ShapeDtypeStruct((4, 4, 2, 4, rows, width), tokens.dtype)
     return pl.pallas_call(
         gather_kernel,
-        out_shape=(shape, shape),
-        in_specs=[pl.BlockSpec(memory_space=pltpu.VMEM)] * 2,
-        out_specs=[pl.BlockSpec(memory_space=pl.ANY)] * 2,
+        out_shape=(shape, shape, jax.ShapeDtypeStruct((4, 4, 2) + meta.shape, meta.dtype)),
+        in_specs=[pl.BlockSpec(memory_space=pltpu.VMEM)] * 3,
+        out_specs=[pl.BlockSpec(memory_space=pl.ANY)] * 3,
         scratch_shapes=[
             pltpu.SemaphoreType.DMA((2, 3, 40)),
             pltpu.SemaphoreType.DMA((2, 3, 40)),
-            pltpu.SemaphoreType.DMA((2,)),
+            pltpu.SemaphoreType.DMA((8,)),
+            pltpu.SemaphoreType.DMA((8,)),
+            pltpu.SemaphoreType.DMA((3,)),
         ],
         compiler_params=pltpu.CompilerParams(collective_id=0, has_side_effects=True),
-    )(tokens, out_grad)
+    )(tokens, out_grad, meta)
 
 CAPS = 24
 
 
-def pair_selectors(ids, probs, first):
-    groups, top, toks = ids.shape
+def pair_selectors(meta, first):
+    top, toks = meta.shape[1] // 2, meta.shape[2]
+    ids, probs = meta[:, :top].astype(jnp.int32), meta[:, top:]
     before = (lax.broadcasted_iota(jnp.int32, (toks, toks), 0) < lax.broadcasted_iota(jnp.int32, (toks, toks), 1)).astype(jnp.bfloat16)
     out = []
     for e in range(2):
@@ -199,7 +239,7 @@
     return out
 
 
-def expert_kernel(ids_ref, probs_ref, x_ref, dy_ref, wg_ref, wu_ref, wd_ref, out_ref, pg_ref,
+def expert_kernel(meta_ref, x_ref, dy_ref, wg_ref, wu_ref, wd_ref, out_ref, pg_ref,
                   xr, dr, rp, pw, pr, *, sets, per_set):
     step = pl.program_id(0)
     first = lax.axis_index("ctx") * 2
@@ -213,7 +253,7 @@
         i = step - per_set
         at = pl.multiple_of(lax.rem(i, per_set) * 2 * CAPS, 16)
         pair = pl.ds(2 * i, 2)
-        chosen = pair_selectors(ids_ref[pair], probs_ref[pair], first)
+        chosen = pair_selectors(meta_ref[pair], first)
         both = jnp.concatenate([c[0] for c in chosen], axis=0).astype(jnp.bfloat16)
         for q in range(quarters):
             cols = pl.ds(q * width, width)
@@ -235,7 +275,7 @@
     def _():
         at = pl.multiple_of(lax.rem(step, per_set) * 2 * CAPS, 16)
         pair = pl.ds(2 * step, 2)
-        chosen = pair_selectors(ids_ref[pair], probs_ref[pair], first)
+        chosen = pair_selectors(meta_ref[pair], first)
         both = jnp.concatenate([c[0] for c in chosen], axis=0).astype(jnp.bfloat16)
         for src, dst in ((x_ref, xr), (dy_ref, dr)):
             for q in range(quarters):
@@ -270,7 +310,7 @@
                 rp[e, :, cols] = part.astype(jnp.bfloat16)
 
 
-def expert_pass(ids, probs, gx, gy, wg, wu, wd):
+def expert_pass(meta, gx, gy, wg, wu, wd):
     groups, quarters, toks, width = gx.shape
     depth, ff = wg.shape[1:]
     per_set = 4
@@ -282,10 +322,9 @@
     return pl.pallas_call(
         functools.partial(expert_kernel, sets=sets, per_set=per_set),
         grid=(steps + per_set,),
-        out_shape=(jax.ShapeDtypeStruct(gx.shape, jnp.bfloat16), jax.ShapeDtypeStruct((groups,) + ids.shape[1:], jnp.float32)),
+        out_shape=(jax.ShapeDtypeStruct(gx.shape, jnp.bfloat16), jax.ShapeDtypeStruct((groups, meta.shape[1] // 2, toks), jnp.float32)),
         in_specs=[
-            pl.BlockSpec(ids.shape, zero3),
-            pl.BlockSpec(probs.shape, zero3),
+            pl.BlockSpec(meta.shape, zero3),
             pl.BlockSpec((2, quarters, toks, width), lambda i: (jnp.minimum(i, steps - 1), 0, 0, 0)),
             pl.BlockSpec((2, quarters, toks, width), lambda i: (jnp.minimum(i, steps - 1), 0, 0, 0)),
             pl.BlockSpec(wg.shape, zero3, pipeline_mode=one),
@@ -294,7 +333,7 @@
         ],
         out_specs=[
             pl.BlockSpec((2, quarters, toks, width), lambda i: (jnp.maximum(i - per_set, 0), 0, 0, 0)),
-            pl.BlockSpec((2,) + ids.shape[1:], lambda i: (jnp.maximum(i - per_set, 0), 0, 0)),
+            pl.BlockSpec((2, meta.shape[1] // 2, toks), lambda i: (jnp.maximum(i - per_set, 0), 0, 0)),
         ],
         scratch_shapes=[
             pltpu.VMEM((2, rows, depth), jnp.bfloat16),
@@ -304,14 +343,14 @@
             pltpu.VMEM((2, rows, 128), jnp.float32),
         ],
         compiler_params=pltpu.CompilerParams(vmem_limit_bytes=60 * 1024 * 1024),
-    )(ids, probs, gx, gy, wg, wu, wd)
+    )(meta, gx, gy, wg, wu, wd)
 
 PARTS = ((0, 48), (48, 48), (96, 32))
 
 
-def scatter_kernel(p_ref, out_ref, *scratch):
+def scatter_kernel(p_ref, pg_ref, out_ref, prob_ref, *scratch):
     accs, sibs, fulls, parts, lone_full, lone_part = (scratch[3 * i:3 * i + 3] for i in range(6))
-    send, recv, local = scratch[18:]
+    pacc, psib, pring, pall, psend, precv, send, recv, local = scratch[18:]
     pos, core = my_place()
     entry_barrier(pos, core)
     width = out_ref.shape[1]
@@ -326,6 +365,55 @@
         copy.start()
         started.append(copy)
         return copy
+
+    def prob_program():
+        def go(i, source, target, device):
+            copy = pltpu.make_async_remote_copy(
+                src_ref=source, dst_ref=target, send_sem=psend.at[i], recv_sem=precv.at[i],
+                device_id=device, device_id_type=MESH)
+            copy.start()
+            started.append(copy)
+            return copy
+
+        load = pltpu.make_async_copy(pg_ref.at[:, :, core], pacc, local.at[3, 0])
+        load.start()
+        push = go(0, pg_ref.at[:, :, 1 - core], psib, device_of(pos, 1 - core))
+        yield
+        load.wait()
+        push.wait_recv()
+        for i in range(4):
+            pacc[i] = pacc[i] + psib[i]
+        n = 1
+        for stage, axis in enumerate("zy"):
+            def spot(by):
+                at = shifted(pos, axis, by)
+                return (slice(None), at["z"]) if axis == "z" else (pl.ds(at["y"], 1), at["z"])
+            size = 4 if axis == "z" else 1
+            ring = [pring.at[stage, i, pl.ds(0, size)] for i in range(3)]
+            plus, minus = device_of(shifted(pos, axis, 1), core), device_of(shifted(pos, axis, 3), core)
+            far = go(n, pacc.at[spot(2)], ring[0], plus)
+            yield
+            far.wait_recv()
+            pacc[spot(1)] = pacc[spot(1)] + ring[0][...]
+            one = go(n + 1, pacc.at[spot(1)], ring[1], plus)
+            two = go(n + 2, pacc.at[spot(3)], ring[2], minus)
+            yield
+            one.wait_recv()
+            two.wait_recv()
+            pacc[spot(0)] = pacc[spot(0)] + ring[1][...] + ring[2][...]
+            n += 3
+        pall[pos["x"]] = pacc[pos["y"], pos["z"]]
+        here = pall.at[pos["x"]]
+        one = go(n, here, here, device_of(shifted(pos, "x", 1), core))
+        two = go(n + 1, here, here, device_of(shifted(pos, "x", 3), core))
+        yield
+        one.wait_recv()
+        back = pall.at[shifted(pos, "x", 3)["x"]]
+        far = go(n + 2, back, back, device_of(shifted(pos, "x", 1), core))
+        two.wait_recv()
+        yield
+        far.wait_recv()
+        prob_ref[...] = pall[0] + pall[1] + pall[2] + pall[3]
 
     def program(color):
         a, b, c = ORDERS[color]
@@ -467,7 +555,7 @@
             add_one(0, slice(None), lone_full[color][side])
         out_ref[rows, :] = acc[where(pos, ())]
 
-    live = [program(color) for color in range(3)]
+    live = [prob_program()] + [program(color) for color in range(3)]
     while live:
         still = []
         for prog in live:
@@ -481,7 +569,7 @@
         s.wait_send()
 
 
-def scatter_all(dense):
+def scatter_all(dense, pg):
     rows, width = dense.shape[-2:]
     half = width // 2
     bf = jnp.bfloat16
@@ -497,29 +585,32 @@
         scratch += [pltpu.VMEM(make(n), bf) for _, n in PARTS]
     return pl.pallas_call(
         scatter_kernel,
-        out_shape=jax.ShapeDtypeStruct((rows, width), bf),
-        in_specs=[pl.BlockSpec(memory_space=pl.ANY)],
-        out_specs=pl.BlockSpec(memory_space=pltpu.VMEM),
+        out_shape=(jax.ShapeDtypeStruct((rows, width), bf), jax.ShapeDtypeStruct(pg.shape[3:], pg.dtype)),
+        in_specs=[pl.BlockSpec(memory_space=pl.ANY)] * 2,
+        out_specs=[pl.BlockSpec(memory_space=pltpu.VMEM)] * 2,
         scratch_shapes=scratch + [
+            pltpu.VMEM((4, 4) + pg.shape[3:], pg.dtype),
+            pltpu.VMEM((4, 4) + pg.shape[3:], pg.dtype),
+            pltpu.VMEM((2, 3, 4) + pg.shape[3:], pg.dtype),
+            pltpu.VMEM((4,) + pg.shape[3:], pg.dtype),
+            pltpu.SemaphoreType.DMA((10,)),
+            pltpu.SemaphoreType.DMA((10,)),
             pltpu.SemaphoreType.DMA((3, 40)),
             pltpu.SemaphoreType.DMA((3, 40)),
-            pltpu.SemaphoreType.DMA((3, 16)),
+            pltpu.SemaphoreType.DMA((4, 16)),
         ],
         compiler_params=pltpu.CompilerParams(collective_id=1, has_side_effects=True, vmem_limit_bytes=62 * 1024 * 1024),
-    )(dense)
+    )(dense, pg)
 
 
 def on_device(tokens, out_grad, router_probs, expert_ids, w_gate, w_up, w_down):
     toks, width = tokens.shape
-    gx, gy = gather_all(tokens, out_grad)
-    ids = lax.all_gather(expert_ids.T, "ctx", axis=0)
-    probs = lax.all_gather(router_probs.T, "ctx", axis=0).astype(jnp.float32)
+    meta = jnp.concatenate([expert_ids.T.astype(jnp.float32), router_probs.T.astype(jnp.float32)], axis=0)
+    gx, gy, gm = gather_all(tokens, out_grad, meta)
     flat = (32, 4, toks, width)
-    dense, pg = expert_pass(ids, probs, gx.reshape(flat), gy.reshape(flat), w_gate, w_up, w_down)
-    token_grad = scatter_all(dense.reshape(gx.shape))
-    pg = lax.psum_scatter(pg, "ctx", scatter_dimension=0, tiled=True)
-    pg = lax.psum(pg, "tp")
-    return token_grad, pg[0].T.astype(jnp.bfloat16)
+    dense, pg = expert_pass(gm.reshape((32,) + meta.shape), gx.reshape(flat), gy.reshape(flat), w_gate, w_up, w_down)
+    token_grad, prob_grad = scatter_all(dense.reshape(gx.shape), pg.reshape((4, 4, 2) + pg.shape[1:]))
+    return token_grad, prob_grad.T.astype(jnp.bfloat16)
 
 
 def solution(mesh):

time: 415 us -> 332 us (0.80)
  blocking collectives: 62.7 us -> 0 us
  waiting for transfers between devices: 14.7 us -> 0 us
  between operations: 14.1 us -> 0.65 us
  Pallas kernels: 318 us -> 326 us
    all_gather x2 -> x0, blocking collectives: 51.7 us -> none  [the longest x1 25.9 us: on_device(): ids = lax.all_gather(expert_ids.T, 'ctx', axis=0)]
    unnamed x2 -> x0, waiting for transfers between devices: 14.7 us -> none
    psum x1 -> x0, blocking collectives: 11 us -> none  [on_device(): pg = lax.psum(pg, 'tp')]
    pallas_call x2, Pallas kernels: 229 us -> 237 us  [the longest x1 148 us: gather_all(): pl.pallas_call(gather_kernel, out_shape=(shape, shape, jax.ShapeDtypeStru...]
  transfers between devices with their start and end apart: 1 -> 0, of which waited for: 1 -> 0; matrix products, arithmetic and copies ran while one was open for 0% -> 0% of each run, Pallas kernels for 20% -> 0%
where the time goes in v2:
time: 332 us; the launch traced here: 331 us
  Pallas kernels  326 us (98%)
    pallas_call x1, Pallas kernels, gather_all(): pl.pallas_call(gather_kernel, out_shape=(shape, shape, jax.ShapeDtypeStru...  148 us
    pallas_call x1, Pallas kernels, expert_pass(): pl.pallas_call(functools.partial(expert_kernel, sets=sets, per_set=per_se...  89.2 us
    pallas_call x1, Pallas kernels, scatter_all(): pl.pallas_call(scatter_kernel, out_shape=(jax.ShapeDtypeStruct((rows, wid...  88.7 us

profile of v2, /device:TPU:0, one launch (start us, length us, event | category | flops | bytes accessed | tf_op | source)
XLA Modules:
  0.0 331.4 jit_solution(2953650467965709552)
XLA Ops:
  0.6 0.7 convert_bitcast_fusion
  1.3 0.7 convert_bitcast_fusion.1
  2.0 0.6 pad_maximum_fusion.meta_ref
  2.6 148.0 %shard_map.86 = (bf16[4,4,2,4,128,1024]{5,4,3,2,1,0:T(8,128)(2,1)}, bf16[4,4,2,4,128,1024]{5,4,3,2,1,0:T(8,128)(2,1)}, f32[4,4,2,16,128]{4,3,2,1,0:T(8,128)}) custom-call(bf16[128,1024]{1,0:T(8,128)(2,1)} %tok_ref.1, bf16[128,1024]{1,0:T(8,128)(2,1)} %dy_ref.1, f32[16,128]{1,0:T(8,128)} %pad_maximum_fusion.meta_ref), custom_call_target="tpu_custom_call" | custom-call | tf_op jit(solution)/shard_map/pallas_call | solution.py:200
  150.6 89.2 %shard_map.87 = (bf16[32,4,128,1024]{3,2,1,0:T(8,128)(2,1)}, f32[32,8,128]{2,1,0:T(8,128)}) custom-call(f32[32,16,128]{2,1,0:T(8,128)} %bitcast.14, bf16[32,4,128,1024]{3,2,1,0:T(8,128)(2,1)} %bitcast.12, bf16[32,4,128,1024]{3,2,1,0:T(8,128)(2,1)} %bitcast.13, bf16[2,4096,384]{2,1,0:T(8,128)(2,1)} %wg_ref.1, bf16[2,4096,384]{2,1,0:T(8,128)(2,1)} %wu_ref.1, ...), custom_call_target="tpu_custom_call" | custom-call | tf_op jit(solution)/shard_map/pallas_call | solution.py:322
  239.8 88.7 %shard_map.88 = (bf16[128,1024]{1,0:T(8,128)(2,1)}, f32[8,128]{1,0:T(8,128)}) custom-call(bf16[4,4,2,4,128,1024]{5,4,3,2,1,0:T(8,128)(2,1)} %bitcast.11, f32[4,4,2,8,128]{4,3,2,1,0:T(8,128)} %bitcast.15), custom_call_target="tpu_custom_call" | custom-call | tf_op jit(solution)/shard_map/pallas_call | solution.py:586
  328.5 1.3 convert_bitcast_fusion.2
  329.8 1.7 copy.10

commit v3 on v2

v3 whole, which is shorter than its diff:
```python
import functools
import jax
import jax.numpy as jnp
from jax import lax
from jax.experimental import pallas as pl
from jax.experimental.pallas import tpu as pltpu
from jax.sharding import PartitionSpec as P

MESH = pl.DeviceIdType.MESH
ORDERS = (("x", "y", "z"), ("y", "z", "x"), ("z", "x", "y"))
SPLITS = (((0, 40), (40, 40), (80, 48)), ((0, 48), (48, 40), (88, 40)))


def my_place():
    ctx = lax.axis_index("ctx")
    return {"x": lax.axis_index("tp"), "y": ctx // 8, "z": (ctx // 2) % 4}, ctx % 2


def device_of(pos, core):
    return ((pos["y"] * 4 + pos["z"]) * 2 + core, pos["x"])


def shifted(pos, axis, by):
    other = dict(pos)
    other[axis] = (pos[axis] + by) % 4
    return other


def entry_barrier(pos, core):
    barrier = pltpu.get_barrier_semaphore()
    for axis in "xyz":
        for by in (1, 3):
            pl.semaphore_signal(barrier, inc=1, device_id=device_of(shifted(pos, axis, by), core), device_id_type=MESH)
    pl.semaphore_signal(barrier, inc=1, device_id=device_of(pos, 1 - core), device_id_type=MESH)
    pl.semaphore_wait(barrier, 7)


CAPS = 24
LAG = 8
PER_TICK = 4
PREP = 4


def pair_selectors(meta, first):
    top, toks = meta.shape[1] // 2, meta.shape[2]
    ids, probs = meta[:, :top].astype(jnp.int32), meta[:, top:]
    before = (lax.broadcasted_iota(jnp.int32, (toks, toks), 0) < lax.broadcasted_iota(jnp.int32, (toks, toks), 1)).astype(jnp.bfloat16)
    out = []
    for e in range(2):
        masks, hits, slots, weights = [], [], [], []
        for g in range(2):
            mask = (ids[g] == first + e).astype(jnp.float32)
            hit = jnp.sum(mask, axis=0, keepdims=True)
            slot = jnp.dot(jnp.broadcast_to(hit, (8, toks)).astype(jnp.bfloat16), before, preferred_element_type=jnp.float32)[0:1]
            masks.append(mask)
            hits.append(hit)
            slots.append(slot + float(CAPS * g))
            weights.append(jnp.sum(mask * probs[g], axis=0, keepdims=True))
        hit = jnp.concatenate(hits, axis=1)
        slot = jnp.concatenate(slots, axis=1)
        weight = jnp.concatenate(weights, axis=1)
        row = lax.broadcasted_iota(jnp.int32, (2 * CAPS, 2 * toks), 0)
        sel = jnp.where((row == slot.astype(jnp.int32)) & (hit > 0.5), 1.0, 0.0)
        out.append((sel, weight, masks))
    return out


def gather_kernel(both_ref, meta_ref, wg_hbm, wu_hbm, wd_hbm, g_ref, p_ref, pg_ref,
                  gm_ref, wgu, wd, xr, dr, rp, pw, pr, mixes, turned, stage, held, sums, back, grads,
                  send, recv, msend, mrecv, local, load_sem, out_sem):
    pos, core = my_place()
    first = lax.axis_index("ctx") * 2
    toks, width = both_ref.shape[1:]
    ff = wg_hbm.shape[2]
    loads = [pltpu.make_async_copy(src, dst, local.at[2 + n]) for n, (src, dst) in enumerate((
        (wg_hbm, wgu.at[:, :, pl.ds(0, ff)]), (wu_hbm, wgu.at[:, :, pl.ds(ff, ff)]), (wd_hbm, wd)))]
    entry_barrier(pos, core)
    started = []
    own = pltpu.make_async_copy(both_ref.at[core], g_ref.at[core, pos["y"], pos["z"], core, pos["x"]], local.at[0])
    own.start()
    swap = pltpu.make_async_remote_copy(
        src_ref=both_ref.at[1 - core], dst_ref=g_ref.at[1 - core, pos["y"], pos["z"], core, pos["x"]],
        send_sem=msend.at[7], recv_sem=mrecv.at[7], device_id=device_of(pos, 1 - core), device_id_type=MESH)
    swap.start()
    started.append(swap)
    own_meta = pltpu.make_async_copy(meta_ref, gm_ref.at[pos["y"], pos["z"], core], local.at[1])
    own_meta.start()

    def meta_program():
        def go(i, source, target, device):
            copy = pltpu.make_async_remote_copy(
                src_ref=source, dst_ref=target, send_sem=msend.at[i], recv_sem=mrecv.at[i],
                device_id=device, device_id_type=MESH)
            copy.start()
            started.append(copy)
            return copy

        here = gm_ref.at[pos["y"], pos["z"], core]
        one = go(0, meta_ref, here, device_of(shifted(pos, "y", 1), core))
        two = go(1, meta_ref, here, device_of(shifted(pos, "y", 3), core))
        yield
        one.wait_recv()
        back = gm_ref.at[shifted(pos, "y", 3)["y"], pos["z"], core]
        far = go(2, back, back, device_of(shifted(pos, "y", 1), core))
        two.wait_recv()
        yield
        far.wait_recv()
        own_meta.wait()
        here = gm_ref.at[:, pos["z"], core]
        one = go(3, here, here, device_of(shifted(pos, "z", 1), core))
        two = go(4, here, here, device_of(shifted(pos, "z", 3), core))
        yield
        one.wait_recv()
        back = gm_ref.at[:, shifted(pos, "z", 3)["z"], core]
        far = go(5, back, back, device_of(shifted(pos, "z", 1), core))
        two.wait_recv()
        yield
        far.wait_recv()
        mine = gm_ref.at[:, :, core]
        last = go(6, mine, mine, device_of(pos, 1 - core))
        yield
        last.wait_recv()

    def program(t, color):
        dst = g_ref.at[core]
        a, b, c = ORDERS[color]
        r0, rn = SPLITS[t][color]
        rows = pl.ds(r0, rn)

        def slot(at, whole, part=None):
            index = {k: (slice(None) if k in whole else at[k]) for k in "xyz"}
            some = rows
            if part is not None and whole:
                index[a] = pl.ds(2 * part, 2)
            elif part is not None:
                some = pl.ds(r0, 24) if part == 0 else pl.ds(r0 + 24, rn - 24)
            return dst.at[index["y"], index["z"], t, index["x"], some]

        def go(i, source, target, device):
            copy = pltpu.make_async_remote_copy(
                src_ref=source, dst_ref=target, send_sem=send.at[t, color, i],
                recv_sem=recv.at[t, color, i], device_id=device, device_id_type=MESH)
            copy.start()
            started.append(copy)
            return copy

        def block_out(i, at, whole, axis, source=None):
            here = slot(at, whole)
            from_ref = here if source is None else source
            return (go(i, from_ref, here, device_of(shifted(pos, axis, 1), core)),
                    go(i + 1, from_ref, here, device_of(shifted(pos, axis, 3), core)))

        def relay(i, at, whole, axis, pair):
            pair[0].wait_recv()
            piece = slot(shifted(at, axis, 3), whole, 0)
            one = go(i + 2, piece, piece, device_of(shifted(pos, axis, 1), core))
            pair[1].wait_recv()
            piece = slot(shifted(at, axis, 1), whole, 1)
            two = go(i + 3, piece, piece, device_of(shifted(pos, axis, 3), core))
            return one, two

        sib_count = [0]
        sibs = []

        def sibling(at):
            piece = slot(at, (a,))
            sibs.append(go(24 + sib_count[0], piece, piece, device_of(pos, 1 - core)))
            sib_count[0] += 1

        pair = block_out(0, pos, (), a)
        yield
        far = relay(0, pos, (), a, pair)
        yield
        for f in far:
            f.wait_recv()
        pair = block_out(4, pos, (a,), b)
        lasts = [(8, pos, block_out(8, pos, (a,), c))]
        sibling(pos)
        yield
        far = relay(4, pos, (a,), b, pair)
        for n, by in ((12, 3), (16, 1)):
            at = shifted(pos, b, by)
            lasts.append((n, at, block_out(n, at, (a,), c)))
            sibling(at)
        yield
        for f in far:
            f.wait_recv()
        at = shifted(pos, b, 2)
        lasts.append((20, at, block_out(20, at, (a,), c)))
        sibling(at)
        fars = []
        for n, at, pair in lasts:
            yield
            fars.append((at, relay(n, at, (a,), c, pair)))
            sibling(shifted(at, c, 3))
            sibling(shifted(at, c, 1))
            if len(fars) > 1:
                at2, far = fars[-2]
                for f in far:
                    f.wait_recv()
                sibling(shifted(at2, c, 2))
        yield
        at2, far = fars[-1]
        for f in far:
            f.wait_recv()
        sibling(shifted(at2, c, 2))
        yield
        for s in sibs:
            s.wait_recv()


    pairs = [(p // 2, 2 * (p % 2)) for p in range(8)]

    def prepare():
        for w in range(2):
            for p, (y, z) in enumerate(pairs):
                chosen = pair_selectors(gm_ref[y, pl.ds(z, 2), w], first)
                mix = jnp.concatenate([c[0] for c in chosen], axis=0)
                mixes[w, p] = mix.astype(jnp.bfloat16)
                turned[w, p] = mix.T.astype(jnp.bfloat16)
                for e in range(2):
                    col = jnp.sum(chosen[e][0] * chosen[e][1], axis=1, keepdims=True)
                    pw[w, e, pl.ds(p * 2 * CAPS, 2 * CAPS), :] = jnp.broadcast_to(col, (2 * CAPS, 128))
                yield

    def experts(w):
        copies = {}

        def fetch(n):
            y, z = pairs[n // 2]
            copies[n] = pltpu.make_async_copy(g_ref.at[n % 2, y, pl.ds(z, 2), w], stage.at[n % 2], load_sem.at[n % 2])
            copies[n].start()

        fetch(0)
        fetch(1)
        for p, (y, z) in enumerate(pairs):
            at = pl.ds(p * 2 * CAPS, 2 * CAPS)
            for t, dst in enumerate((xr, dr)):
                n = 2 * p + t
                copies[n].wait()

                def pick(q, carry):
                    two = stage[t, :, q].reshape(2 * toks, width)
                    rows = jnp.dot(mixes[w, p], two, preferred_element_type=jnp.float32).astype(jnp.bfloat16)
                    cols = pl.ds(pl.multiple_of(q * width, width), width)
                    for e in range(2):
                        dst[e, at, cols] = rows[e * 2 * CAPS:(e + 1) * 2 * CAPS]
                    return carry
                lax.fori_loop(0, 4, pick, 0)
                if n + 2 < 16:
                    fetch(n + 2)
            yield
        if w == 0:
            for load in loads:
                load.wait()
        for e in range(2):
            def product(into, rows, weight, dims):
                into[...] = jnp.zeros_like(into)

                def body(k, carry):
                    cols = pl.ds(pl.multiple_of(k * width, width), width)
                    other = weight[e, cols, :] if dims == 0 else weight[e, :, cols]
                    into[...] += lax.dot_general(rows[e, :, cols], other, (((1,), (dims,)), ((), ())), preferred_element_type=jnp.float32)
                    return carry
                lax.fori_loop(0, 4, body, 0)

            product(sums, xr, wgu, 0)
            yield
            product(back, dr, wd, 1)
            yield
            gate, ups, backs = sums[:, :ff], sums[:, ff:], back[...]
            sig = jax.nn.sigmoid(gate)
            gated = gate * sig
            pr[e] = jnp.broadcast_to(jnp.sum(gated * ups * backs, axis=1, keepdims=True), pr.shape[1:])
            scaled = pw[w, e, :, 0:1] * backs
            grads[:, :ff] = (scaled * ups * sig * (1.0 + gate * (1.0 - sig))).astype(jnp.bfloat16)
            grads[:, ff:] = (scaled * gated).astype(jnp.bfloat16)

            def spread(k, carry):
                cols = pl.ds(pl.multiple_of(k * width, width), width)
                dims = (((1,), (1,)), ((), ()))
                part = lax.dot_general(grads[...], wgu[e, cols, :], dims, preferred_element_type=jnp.float32)
                rp[e, :, cols] = part.astype(jnp.bfloat16)
                return carry
            lax.fori_loop(0, 2, spread, 0)
            yield
            lax.fori_loop(2, 4, spread, 0)
            yield
        outs = []
        for p, (y, z) in enumerate(pairs):
            at = pl.ds(p * 2 * CAPS, 2 * CAPS)
            if p >= 2:
                outs[p - 2].wait()
            slot = p % 2

            def emit(q, carry):
                cols = pl.ds(pl.multiple_of(q * width, width), width)
                rows = jnp.concatenate([rp[e, at, cols] for e in range(2)], axis=0)
                dense = jnp.dot(turned[w, p], rows, preferred_element_type=jnp.float32).astype(jnp.bfloat16)
                for g in range(2):
                    held[slot, g, q] = dense[g * toks:(g + 1) * toks]
                return carry
            lax.fori_loop(0, 4, emit, 0)
            copy = pltpu.make_async_copy(held.at[slot], p_ref.at[y, pl.ds(z, 2), w], out_sem.at[slot])
            copy.start()
            outs.append(copy)
            total = [0.0, 0.0]
            for e in range(2):
                sel = mixes[w, p, pl.ds(e * 2 * CAPS, 2 * CAPS)].astype(jnp.float32)
                value = jnp.sum(sel * pr[e, at, 0:1], axis=0, keepdims=True)
                for g in range(2):
                    mask = (gm_ref[y, z + g, w, :pg_ref.shape[3]].astype(jnp.int32) == first + e).astype(jnp.float32)
                    total[g] = total[g] + mask * value[:, g * toks:(g + 1) * toks]
            for g in range(2):
                pg_ref[y, z + g, w] = total[g]
            yield
        for copy in outs[-2:]:
            copy.wait()

    own.wait()
    swap.wait_recv()
    gathers = [[program(w, color) for color in range(3)] for w in range(2)]
    meta_run = [meta_program()]

    def advance(group):
        group[:] = [g for g in group if next(g, "done") != "done"]

    tick = 0
    prep = [prepare()]
    while gathers[0]:
        for _ in range(0 if meta_run else PREP):
            advance(prep)
        advance(meta_run)
        advance(gathers[0])
        if tick == 3:
            for load in loads:
                load.start()
        if tick >= LAG:
            advance(gathers[1])
        tick += 1
    while prep:
        advance(prep)
    work = [experts(0)]
    while gathers[1] or work:
        for _ in range(PER_TICK if gathers[1] else 100):
            advance(work)
        advance(gathers[1])
    work = [experts(1)]
    while work:
        advance(work)
    for s in started:
        s.wait_send()


def gather_all(both, meta, wg, wu, wd):
    toks, width = both.shape[1:]
    bf, f32 = jnp.bfloat16, jnp.float32
    depth, ff = wg.shape[1:]
    rows = 16 * CAPS
    top = meta.shape[0] // 2
    any_, vm = pl.BlockSpec(memory_space=pl.ANY), pl.BlockSpec(memory_space=pltpu.VMEM)
    return pl.pallas_call(
        gather_kernel,
        out_shape=(
            jax.ShapeDtypeStruct((2, 4, 4, 2, 4, toks, width), bf),
            jax.ShapeDtypeStruct((4, 4, 2, 4, toks, width), bf),
            jax.ShapeDtypeStruct((4, 4, 2, top, toks), f32),
        ),
        in_specs=[vm, vm, any_, any_, any_],
        out_specs=[any_, any_, vm],
        scratch_shapes=[
            pltpu.VMEM((4, 4, 2) + meta.shape, meta.dtype),
            pltpu.VMEM((2, depth, 2 * ff), bf), pltpu.VMEM(wd.shape, bf),
            pltpu.VMEM((2, rows, depth), bf), pltpu.VMEM((2, rows, depth), bf), pltpu.VMEM((2, rows, depth), bf),
            pltpu.VMEM((2, 2, rows, 128), f32), pltpu.VMEM((2, rows, 128), f32),
            pltpu.VMEM((2, 8, 4 * CAPS, 2 * toks), bf), pltpu.VMEM((2, 8, 2 * toks, 4 * CAPS), bf),
            pltpu.VMEM((2, 2, 4, toks, width), bf), pltpu.VMEM((2, 2, 4, toks, width), bf),
            pltpu.VMEM((rows, 2 * ff), f32), pltpu.VMEM((rows, ff), f32), pltpu.VMEM((rows, 2 * ff), bf),
            pltpu.SemaphoreType.DMA((2, 3, 40)), pltpu.SemaphoreType.DMA((2, 3, 40)),
            pltpu.SemaphoreType.DMA((8,)), pltpu.SemaphoreType.DMA((8,)),
            pltpu.SemaphoreType.DMA((5,)), pltpu.SemaphoreType.DMA((2,)), pltpu.SemaphoreType.DMA((2,)),
        ],
        compiler_params=pltpu.CompilerParams(collective_id=0, has_side_effects=True, vmem_limit_bytes=62 * 1024 * 1024),
    )(both, meta, wg, wu, wd)

PARTS = ((0, 48), (48, 48), (96, 32))


def scatter_kernel(p_ref, pg_ref, out_ref, prob_ref, *scratch):
    accs, sibs, fulls, parts, lone_full, lone_part = (scratch[3 * i:3 * i + 3] for i in range(6))
    pacc, psib, pring, pall, psend, precv, send, recv, local = scratch[18:]
    pos, core = my_place()
    entry_barrier(pos, core)
    width = out_ref.shape[1]
    half = width // 2
    cuts = (pl.ds(0, half), pl.ds(half, half))
    started = []

    def go(color, i, source, target, device):
        copy = pltpu.make_async_remote_copy(
            src_ref=source, dst_ref=target, send_sem=send.at[color, i],
            recv_sem=recv.at[color, i], device_id=device, device_id_type=MESH)
        copy.start()
        started.append(copy)
        return copy

    def prob_program():
        def go(i, source, target, device):
            copy = pltpu.make_async_remote_copy(
                src_ref=source, dst_ref=target, send_sem=psend.at[i], recv_sem=precv.at[i],
                device_id=device, device_id_type=MESH)
            copy.start()
            started.append(copy)
            return copy

        load = pltpu.make_async_copy(pg_ref.at[:, :, core], pacc, local.at[3, 0])
        load.start()
        push = go(0, pg_ref.at[:, :, 1 - core], psib, device_of(pos, 1 - core))
        yield
        load.wait()
        push.wait_recv()
        for i in range(4):
            pacc[i] = pacc[i] + psib[i]
        n = 1
        for stage, axis in enumerate("zy"):
            def spot(by):
                at = shifted(pos, axis, by)
                return (slice(None), at["z"]) if axis == "z" else (pl.ds(at["y"], 1), at["z"])
            size = 4 if axis == "z" else 1
            ring = [pring.at[stage, i, pl.ds(0, size)] for i in range(3)]
            plus, minus = device_of(shifted(pos, axis, 1), core), device_of(shifted(pos, axis, 3), core)
            far = go(n, pacc.at[spot(2)], ring[0], plus)
            yield
            far.wait_recv()
            pacc[spot(1)] = pacc[spot(1)] + ring[0][...]
            one = go(n + 1, pacc.at[spot(1)], ring[1], plus)
            two = go(n + 2, pacc.at[spot(3)], ring[2], minus)
            yield
            one.wait_recv()
            two.wait_recv()
            pacc[spot(0)] = pacc[spot(0)] + ring[1][...] + ring[2][...]
            n += 3
        pall[pos["x"]] = pacc[pos["y"], pos["z"]]
        here = pall.at[pos["x"]]
        one = go(n, here, here, device_of(shifted(pos, "x", 1), core))
        two = go(n + 1, here, here, device_of(shifted(pos, "x", 3), core))
        yield
        one.wait_recv()
        back = pall.at[shifted(pos, "x", 3)["x"]]
        far = go(n + 2, back, back, device_of(shifted(pos, "x", 1), core))
        two.wait_recv()
        yield
        far.wait_recv()
        prob_ref[...] = pall[0] + pall[1] + pall[2] + pall[3]

    def program(color):
        a, b, c = ORDERS[color]
        rows = pl.ds(*PARTS[color])
        acc, sib = accs[color], sibs[color]

        def where(at, whole):
            index = {k: (slice(None) if k in whole else at[k]) for k in "xyz"}
            return index["y"], index["z"], index["x"]

        def line(at, part=None):
            index = dict(zip("yzx", where(at, (a,))))
            if part is not None:
                index[a] = pl.ds(2 * part, 2)
            return acc.at[index["y"], index["z"], index["x"]]

        def add_line(at, part, other):
            low, high = (0, 4) if part is None else (2 * part, 2 * part + 2)

            def body(i, carry):
                mine = dict(at)
                mine[a] = i
                spot = where(mine, ())
                acc[spot] = acc[spot] + other(i - low)
                return carry
            lax.fori_loop(low, high, body, 0)

        loads = {}
        order = (2, 1, 3, 0)
        count = 0
        for j in order:
            for k in order:
                at = shifted(shifted(pos, b, j), c, k)
                y, z, x = where(at, (a,))
                load = pltpu.make_async_copy(p_ref.at[y, z, core, x, rows], line(at), local.at[color, count])
                load.start()
                push = go(color, 24 + count, p_ref.at[y, z, 1 - core, x, rows], sib.at[y, z, x], device_of(pos, 1 - core))
                loads[j, k] = (at, load, push)
                count += 1
            yield

        def merge(j, k):
            at, load, push = loads[j, k]
            load.wait()
            push.wait_recv()

            def other(i):
                mine = dict(at)
                mine[a] = i
                return sib[where(mine, ())]
            add_line(at, None, other)

        def first(n, axis, unit):
            return (go(color, n * 4, unit(2, 0), parts[color].at[n, 0], device_of(shifted(pos, axis, 1), core)),
                    go(color, n * 4 + 1, unit(2, 1), parts[color].at[n, 1], device_of(shifted(pos, axis, 3), core)))

        def second(n, axis, unit, add, halves):
            sent = []
            for side, by in ((0, 1), (1, 3)):
                halves[side].wait_recv()
                add(by, side, lambda i, side=side: parts[color][n, side, i])
                sent.append(go(color, n * 4 + 2 + side, unit(by, None), fulls[color].at[n, side],
                               device_of(shifted(pos, axis, by), core)))
            return sent

        def third(n, add, sent):
            for side in range(2):
                sent[side].wait_recv()
                add(0, None, lambda i, side=side: fulls[color][n, side, i])

        def last_unit(j):
            return (lambda k, cols: line(shifted(shifted(pos, b, j), c, k), cols),
                    lambda k, cols, other: add_line(shifted(shifted(pos, b, j), c, k), cols, other))

        halves, sents = {}, {}

        def stage_a(n):
            merge(order[n], 2)
            halves[n] = first(n, c, last_unit(order[n])[0])

        def stage_b(n):
            merge(order[n], 1)
            merge(order[n], 3)
            unit, add = last_unit(order[n])
            sents[n] = second(n, c, unit, add, halves[n])

        def stage_c(n):
            merge(order[n], 0)
            third(n, last_unit(order[n])[1], sents[n])

        mid_unit = lambda k, cols: line(shifted(pos, b, k), cols)
        mid_add = lambda k, cols, other: add_line(shifted(pos, b, k), cols, other)
        stage_a(0)
        yield
        stage_a(1)
        yield
        stage_b(0)
        yield
        stage_a(2)
        yield
        stage_b(1)
        yield
        stage_c(0)
        mid_halves = first(4, b, mid_unit)
        yield
        stage_a(3)
        yield
        stage_b(2)
        yield
        stage_c(1)
        yield
        stage_b(3)
        yield
        stage_c(2)
        mid_sent = second(4, b, mid_unit, mid_add, mid_halves)
        yield
        stage_c(3)
        third(4, mid_add, mid_sent)
        yield

        def one(at, cols=slice(None)):
            return acc.at[(*where(at, ()), slice(None), cols)]

        def add_one(by, cols, other):
            spot = (*where(shifted(pos, a, by), ()), slice(None), cols)
            acc[spot] = acc[spot] + other

        tail = [go(color, 20, one(shifted(pos, a, 2), cuts[0]), lone_part[color].at[0], device_of(shifted(pos, a, 1), core)),
                go(color, 21, one(shifted(pos, a, 2), cuts[1]), lone_part[color].at[1], device_of(shifted(pos, a, 3), core))]
        yield
        sent = []
        for side, by in ((0, 1), (1, 3)):
            tail[side].wait_recv()
            add_one(by, cuts[side], lone_part[color][side])
            sent.append(go(color, 22 + side, one(shifted(pos, a, by)), lone_full[color].at[side], device_of(shifted(pos, a, by), core)))
        yield
        for side in range(2):
            sent[side].wait_recv()
            add_one(0, slice(None), lone_full[color][side])
        out_ref[rows, :] = acc[where(pos, ())]

    live = [prob_program()] + [program(color) for color in range(3)]
    while live:
        still = []
        for prog in live:
            try:
                next(prog)
                still.append(prog)
            except StopIteration:
                pass
        live = still
    for s in started:
        s.wait_send()


def scatter_all(dense, pg):
    rows, width = dense.shape[-2:]
    half = width // 2
    bf = jnp.bfloat16
    scratch = []
    for make in (
        lambda n: (4, 4, 4, n, width),
        lambda n: (4, 4, 4, n, width),
        lambda n: (5, 2, 4, n, width),
        lambda n: (5, 2, 2, n, width),
        lambda n: (2, n, width),
        lambda n: (2, n, half),
    ):
        scratch += [pltpu.VMEM(make(n), bf) for _, n in PARTS]
    return pl.pallas_call(
        scatter_kernel,
        out_shape=(jax.ShapeDtypeStruct((rows, width), bf), jax.ShapeDtypeStruct(pg.shape[3:], pg.dtype)),
        in_specs=[pl.BlockSpec(memory_space=pl.ANY)] * 2,
        out_specs=[pl.BlockSpec(memory_space=pltpu.VMEM)] * 2,
        scratch_shapes=scratch + [
            pltpu.VMEM((4, 4) + pg.shape[3:], pg.dtype),
            pltpu.VMEM((4, 4) + pg.shape[3:], pg.dtype),
            pltpu.VMEM((2, 3, 4) + pg.shape[3:], pg.dtype),
            pltpu.VMEM((4,) + pg.shape[3:], pg.dtype),
            pltpu.SemaphoreType.DMA((10,)),
            pltpu.SemaphoreType.DMA((10,)),
            pltpu.SemaphoreType.DMA((3, 40)),
            pltpu.SemaphoreType.DMA((3, 40)),
            pltpu.SemaphoreType.DMA((4, 16)),
        ],
        compiler_params=pltpu.CompilerParams(collective_id=1, has_side_effects=True, vmem_limit_bytes=62 * 1024 * 1024),
    )(dense, pg)


def on_device(tokens, out_grad, router_probs, expert_ids, w_gate, w_up, w_down):
    toks, width = tokens.shape
    meta = jnp.concatenate([expert_ids.T.astype(jnp.float32), router_probs.T.astype(jnp.float32)], axis=0)
    both = jnp.stack([tokens, out_grad])
    _, dense, pg = gather_all(both, meta, w_gate, w_up, w_down)
    token_grad, prob_grad = scatter_all(dense, pg)
    return token_grad, prob_grad.T.astype(jnp.bfloat16)


def solution(mesh):
    return jax.shard_map(
        on_device,
        mesh=mesh,
        in_specs=(P("ctx", "tp"), P("ctx", "tp"), P("ctx", None), P("ctx", None), P("ctx", None, "tp"), P("ctx", None, "tp"), P("ctx", "tp", None)),
        out_specs=(P("ctx", "tp"), P("ctx", None)),
        check_vma=False,
    )
```

time: 332 us -> 318 us (0.958)
  Pallas kernels: 326 us -> 310 us
    pallas_call x2 -> x1, Pallas kernels: 237 us -> 219 us  [gather_all(): pl.pallas_call(gather_kernel, out_shape=(jax.ShapeDtypeStruct((2, 4, 4, 2...]
where the time goes in v3:
time: 318 us; the launch traced here: 317 us
  Pallas kernels  310 us (97%)
  other arithmetic  5.12 us (2%)
    pallas_call x1, Pallas kernels, gather_all(): pl.pallas_call(gather_kernel, out_shape=(jax.ShapeDtypeStruct((2, 4, 4, 2...  219 us
    pallas_call x1, Pallas kernels, scatter_all(): pl.pallas_call(scatter_kernel, out_shape=(jax.ShapeDtypeStruct((rows, wid...  90.6 us

profile of v3, /device:TPU:0, one launch (start us, length us, event | category | flops | bytes accessed | tf_op | source)
XLA Modules:
  0.0 317.4 jit_solution(10145226370127844406)
XLA Ops:
  0.6 0.7 convert_bitcast_fusion
  1.3 0.7 convert_bitcast_fusion.1
  2.0 0.6 pad_maximum_fusion.1.meta_ref
  2.6 1.9 pad_maximum_fusion.both_ref
  4.5 219.4 %shard_map.86 = (bf16[2,4,4,2,4,128,1024]{6,5,4,3,2,1,0:T(8,128)(2,1)}, bf16[4,4,2,4,128,1024]{5,4,3,2,1,0:T(8,128)(2,1)}, f32[4,4,2,8,128]{4,3,2,1,0:T(8,128)}) custom-call(bf16[2,128,1024]{2,1,0:T(8,128)(2,1)} %pad_maximum_fusion.both_ref, f32[16,128]{1,0:T(8,128)} %pad_maximum_fusion.1.meta_ref, bf16[2,4096,384]{2,1,0:T(8,128)(2,1)} %wg_hbm.1, ...), custom_call_target="tpu_custom_call" | custom-call | tf_op jit(solution)/shard_map/pallas_call | solution.py:362
  223.9 90.6 %shard_map.87 = (bf16[128,1024]{1,0:T(8,128)(2,1)}, f32[8,128]{1,0:T(8,128)}) custom-call(bf16[4,4,2,4,128,1024]{5,4,3,2,1,0:T(8,128)(2,1)} %get-tuple-element.6.p_ref, f32[4,4,2,8,128]{4,3,2,1,0:T(8,128)} %get-tuple-element.7.pg_ref), custom_call_target="tpu_custom_call" | custom-call | tf_op jit(solution)/shard_map/pallas_call | solution.py:624
  314.5 1.3 convert_bitcast_fusion.2
  315.7 1.7 copy.10
